TPU v7x, 256 devices: a whole 4x4x8 slice. The times are simulated.
256 devices in a mesh: rows: 8 (over y, core), chan: 32 (over x, z).
Axes of the slice: x: 4, y: 4, z: 8, core: 2. Of those that a mesh axis runs over, the one named last changes fastest.
Arguments:
- features: bfloat16 [512, 1536, 256], P('rows', 'chan'), may hold values from -6 to 6
- mixing: float32 [3, 512, 256], P(None, 'rows'), may hold values from 0 to 1, as said below
- decay_rate: float32 [512, 256], P('rows'), may hold values from 0 to 0.5, as said below
- gate_input: bfloat16 [512, 1536, 256], P('rows', 'chan'), may hold values from -6 to 6
- out_weight: bfloat16 [1536, 1536], replicated, may hold values from -0.15625 to 0.15625
Outputs:
- projected: bfloat16 [512, 1536, 256], P(('rows', 'chan'))
Inputs may be any that keep to these rules, and one draw needn't show every extreme that they name: `mixing`: at every row and column the three weights are positive where their neighbour exists, the left weight is zero at column 0 and the right weight at column 255, and the three sum to one. `decay_rate`: every entry is positive.
All inputs are finite; a program needn't handle non-finite values.
Results may differ from a plain program's by a relative error of at most 0.0049.
Values may be sent and summed in bfloat16 or wider, within the bound.
No kernel may reach another device: no remote copies, remote signals or barrier semaphores. Data moves between devices by JAX's collectives and lax.ppermute only.
A program may use at most 128 MiB of HBM per device.

v0:
```python
import jax
import jax.numpy as jnp
from jax import lax
from jax.experimental import pallas as pl
from jax.experimental.pallas import tpu as pltpu
from jax.sharding import PartitionSpec as P

STEP_ROWS = 8
HALF = 128
REACH = 32
TILES = 4
VMEM_LIMIT = 16 * 1024 * 1024
HIGHEST = lax.Precision.HIGHEST


def stencil(state, left_w, mid_w, right_w):
    width = state.shape[1]
    before_col = pltpu.roll(state, 1, 1)
    after_col = pltpu.roll(state, width - 1, 1)
    return left_w * before_col + mid_w * state + right_w * after_col


def diagonal(first, count, left, width):
    source = lax.broadcasted_iota(jnp.int32, (count, width), 0) + first
    column = lax.broadcasted_iota(jnp.int32, (count, width), 1) + left
    return jnp.where(source == column, 1.0, 0.0).astype(jnp.float32)


def operator_kernel(
    mix_ref, decay_ref, op_ref, early_ref, late_ref, left_ref, mid_ref, right_ref, in_ref, left_cut_ref, right_cut_ref
):
    rows, width = decay_ref.shape
    decay = decay_ref[...]
    retain = 1.0 - decay
    column = lax.broadcasted_iota(jnp.int32, (rows, width), 1)
    left_w = retain * mix_ref[0]
    right_w = retain * mix_ref[2]
    left_ref[...] = left_w
    mid_ref[...] = retain * mix_ref[1]
    right_ref[...] = right_w
    in_ref[...] = jnp.sqrt(decay)
    left_cut_ref[...] = jnp.where(column == HALF, 0.0, left_w)
    right_cut_ref[...] = jnp.where(column == HALF - 1, 0.0, right_w)

    inner = HALF - REACH
    outs = (early_ref, late_ref)
    for out in outs:
        out[0:inner, HALF:width] = jnp.zeros((inner, width - HALF), jnp.float32)
        out[width - inner : width, 0:HALF] = jnp.zeros((inner, HALF), jnp.float32)

    def sweep(first, count, left, right, lefts, rights):
        lanes = slice(left, right)

        def step(i, states):
            news = []
            for half in range(2):
                row = pl.ds(i + half * REACH, 1)
                weights = [ref[row, :][:, lanes] for ref in (lefts, mid_ref, rights)]
                news.append(stencil(states[half], *weights))
            return tuple(news)

        start = diagonal(first, count, left, right - left)
        finals = lax.fori_loop(0, REACH, step, (start, start), unroll=4)
        for out, final in zip(outs, finals):
            out[first : first + count, lanes] = final

    sweep(0, inner, 0, HALF, left_ref, right_cut_ref)
    sweep(width - inner, inner, HALF, width, left_cut_ref, right_ref)
    sweep(inner, 2 * REACH, 0, width, left_ref, right_ref)
    op_ref[...] = jnp.dot(
        early_ref[...], late_ref[...], precision=HIGHEST, preferred_element_type=jnp.float32
    ).astype(op_ref.dtype)


def operator_of(mixing, decay_rate):
    _, rows, width = mixing.shape
    square = jax.ShapeDtypeStruct((width, width), jnp.float32)
    coef = jax.ShapeDtypeStruct((rows, width), jnp.float32)
    return pl.pallas_call(
        operator_kernel,
        out_shape=(jax.ShapeDtypeStruct((width, width), jnp.bfloat16), square, square, coef, coef, coef, coef),
        scratch_shapes=[pltpu.VMEM((rows, width), jnp.float32)] * 2,
        cost_estimate=pl.CostEstimate(
            flops=5 * rows * width * width, bytes_accessed=8 * rows * width * 4, transcendentals=0
        ),
        compiler_params=pltpu.CompilerParams(vmem_limit_bytes=VMEM_LIMIT),
        name="operator",
    )(mixing, decay_rate)


def ending_kernel(feat_ref, left_ref, mid_ref, right_ref, in_ref, late_ref, early_end_ref, end_ref, state_ref):
    @pl.when(pl.program_id(0) == 0)
    def _():
        state_ref[...] = jnp.zeros_like(state_ref)

    states = [state_ref[0], state_ref[1]]
    for j in range(feat_ref.shape[1]):
        row = pl.ds(j, 1)
        for half in range(2):
            push = in_ref[half, row, :] * feat_ref[half, j].astype(jnp.float32)
            states[half] = (
                stencil(states[half], left_ref[half, row, :], mid_ref[half, row, :], right_ref[half, row, :]) + push
            )
    state_ref[0] = states[0]
    state_ref[1] = states[1]

    @pl.when(pl.program_id(0) == pl.num_programs(0) - 1)
    def _():
        early_end_ref[...] = states[0]
        end_ref[...] = states[1] + jnp.dot(
            states[0], late_ref[...], precision=HIGHEST, preferred_element_type=jnp.float32
        )


def ending(features, coefs, late):
    _, rows, channels, width = features.shape
    coef_spec = pl.BlockSpec((2, STEP_ROWS, width), lambda i: (0, i, 0))
    state = jax.ShapeDtypeStruct((channels, width), jnp.float32)
    state_spec = pl.BlockSpec((channels, width), lambda i: (0, 0))
    return pl.pallas_call(
        ending_kernel,
        grid=(rows // STEP_ROWS,),
        in_specs=[pl.BlockSpec((2, STEP_ROWS, channels, width), lambda i: (0, i, 0, 0))]
        + [coef_spec] * 4
        + [pl.BlockSpec((width, width), lambda i: (0, 0))],
        out_specs=(state_spec, state_spec),
        out_shape=(state, state),
        scratch_shapes=[pltpu.VMEM((2, channels, width), jnp.float32)],
        cost_estimate=pl.CostEstimate(
            flops=14 * rows * channels * width, bytes_accessed=4 * rows * channels * width, transcendentals=0
        ),
        compiler_params=pltpu.CompilerParams(vmem_limit_bytes=VMEM_LIMIT),
        name="ending",
    )(features, *coefs, late)


def applied(state, operator):
    high = state.astype(jnp.bfloat16)
    low = (state - high.astype(jnp.float32)).astype(jnp.bfloat16)
    both = jnp.dot(jnp.concatenate([high, low]), operator, preferred_element_type=jnp.float32)
    return both[: state.shape[0]] + both[state.shape[0] :]


def gated_kernel(
    core_ref, comp_1_ref, comp_2_ref, chip_1_ref, chip_2_ref, chip_3_ref, their_op_ref, their_end_ref,
    early_ref, early_end_ref, feat_ref, gate_ref, left_ref, mid_ref, right_ref, in_ref, out_ref, state_ref,
):
    @pl.when(pl.program_id(0) == 0)
    def _():
        incoming = applied(chip_3_ref[...], comp_2_ref[...]) + chip_2_ref[...]
        incoming = applied(incoming, comp_1_ref[...]) + chip_1_ref[...]
        later = applied(incoming, their_op_ref[...]) + their_end_ref[...]
        incoming = jnp.where(core_ref[0] == 0, incoming, later)
        state_ref[0] = incoming
        state_ref[1] = early_end_ref[...] + jnp.dot(
            incoming, early_ref[...], precision=HIGHEST, preferred_element_type=jnp.float32
        )

    states = [state_ref[0], state_ref[1]]
    for j in range(feat_ref.shape[1]):
        row = pl.ds(j, 1)
        for half in range(2):
            push = in_ref[half, row, :] * feat_ref[half, j].astype(jnp.float32)
            states[half] = (
                stencil(states[half], left_ref[half, row, :], mid_ref[half, row, :], right_ref[half, row, :]) + push
            )
            gate = gate_ref[half, j].astype(jnp.float32)
            out_ref[half, j] = (states[half] * (gate / (1.0 + jnp.exp(-gate)))).astype(out_ref.dtype)
    state_ref[0] = states[0]
    state_ref[1] = states[1]


def gated(core, starts, features, gate_input, coefs):
    _, rows, channels, width = features.shape

    def fixed(array):
        return pl.BlockSpec(array.shape, lambda i, *_: (0,) * array.ndim)

    coef_spec = pl.BlockSpec((2, STEP_ROWS, width), lambda i, *_: (0, i, 0))
    wide_spec = pl.BlockSpec((2, STEP_ROWS, channels, width), lambda i, *_: (0, i, 0, 0))
    return pl.pallas_call(
        gated_kernel,
        grid_spec=pltpu.PrefetchScalarGridSpec(
            num_scalar_prefetch=1,
            grid=(rows // STEP_ROWS,),
            in_specs=[fixed(a) for a in starts] + [wide_spec, wide_spec] + [coef_spec] * 4,
            out_specs=wide_spec,
            scratch_shapes=[pltpu.VMEM((2, channels, width), jnp.float32)],
        ),
        out_shape=jax.ShapeDtypeStruct(features.shape, jnp.bfloat16),
        cost_estimate=pl.CostEstimate(
            flops=24 * rows * channels * width,
            bytes_accessed=12 * rows * channels * width,
            transcendentals=4 * rows * channels * width,
        ),
        compiler_params=pltpu.CompilerParams(vmem_limit_bytes=VMEM_LIMIT),
        name="gated",
    )(core, *starts, features, gate_input, *coefs)


def project_kernel(weight_ref, gated_ref, out_ref, done_ref, sem_ref):
    peers, rows, channels, width = gated_ref.shape
    outs = weight_ref.shape[0]
    tile = outs // TILES
    copies = []
    for row in range(rows):
        here = gated_ref[:, row].reshape(peers * channels, width)
        for t in range(TILES):
            part = pl.ds(t * tile, tile)
            done_ref[row, part, :] = jnp.dot(
                weight_ref[part, :], here, preferred_element_type=jnp.float32
            ).astype(done_ref.dtype)
            copy = pltpu.make_async_copy(done_ref.at[row, part], out_ref.at[row, part], sem_ref.at[row, t])
            copy.start()
            copies.append(copy)
    for copy in copies:
        copy.wait()


def project(out_weight, gathered):
    _, rows, _, width = gathered.shape
    outs = out_weight.shape[0]
    return pl.pallas_call(
        project_kernel,
        in_specs=[pl.BlockSpec(memory_space=pltpu.VMEM)] * 2,
        out_specs=pl.BlockSpec(memory_space=pl.ANY),
        out_shape=jax.ShapeDtypeStruct((rows, outs, width), jnp.bfloat16),
        scratch_shapes=[
            pltpu.VMEM((rows, outs, width), jnp.bfloat16),
            pltpu.SemaphoreType.DMA((rows, TILES)),
        ],
        compiler_params=pltpu.CompilerParams(vmem_limit_bytes=VMEM_LIMIT),
        cost_estimate=pl.CostEstimate(
            flops=2 * rows * outs * outs * width, bytes_accessed=4 * outs * outs, transcendentals=0
        ),
        name="project",
    )(out_weight, gathered)


def shards(slabs, peers, features, mixing, decay_rate, gate_input, out_weight):
    rows, channels, width = features.shape
    features = features.reshape(2, rows // 2, channels, width)
    gate_input = gate_input.reshape(2, rows // 2, channels, width)
    core = lax.axis_index("rows") % 2
    first = core == 0

    def chips_back(value, shift, chip):
        return lax.ppermute(value, "rows", [(i, i + 2 * shift) for i in range(2 * chip, slabs - 2 * shift)])

    def swapped(value):
        return lax.ppermute(value, "rows", [(i, i ^ 1) for i in range(slabs)])

    def in_order(mine, theirs):
        return jnp.where(first, mine, theirs), jnp.where(first, theirs, mine)

    operator, early, late, *coefs = operator_of(mixing, decay_rate)
    coefs = [c.reshape(2, rows // 2, width) for c in coefs]
    their_op = swapped(operator)
    op_0, op_1 = in_order(operator, their_op)
    composite = jnp.dot(op_0, op_1, preferred_element_type=jnp.float32).astype(jnp.bfloat16)
    comp_2 = chips_back(composite, 2, 1)
    comp_1 = chips_back(composite, 1, 1)
    early_end, end = ending(features, coefs, late)
    their_end = swapped(end)
    end_0, end_1 = in_order(end, their_end)
    chip_end = applied(end_0, op_1) + end_1
    chip_3, chip_2, chip_1 = [chips_back(chip_end, shift, 0) for shift in (3, 2, 1)]

    starts = (comp_1, comp_2, chip_1, chip_2, chip_3, their_op, their_end, early, early_end)
    mixed = gated(core.astype(jnp.int32).reshape(1), starts, features, gate_input, coefs)
    mixed = mixed.reshape(peers, rows // peers, channels, width)
    return project(out_weight, lax.all_to_all(mixed, "chan", split_axis=0, concat_axis=0, tiled=True))


def solution(mesh):
    in_specs = (
        P("rows", "chan", None),
        P(None, "rows", None),
        P("rows", None),
        P("rows", "chan", None),
        P(),
    )
    out_specs = P(("rows", "chan"), None, None)

    def whole(features, mixing, decay_rate, gate_input, out_weight):
        return shards(
            mesh.shape["rows"], mesh.shape["chan"], features, mixing, decay_rate, gate_input, out_weight
        )

    return jax.shard_map(whole, mesh=mesh, in_specs=in_specs, out_specs=out_specs, check_vma=False)
```

profile of v0, /device:TPU:48, one launch (start us, length us, event | category | flops | bytes accessed | tf_op | source)
XLA Modules:
  0.0 92.2 jit_solution(14903199523964638970)
XLA Ops:
  0.0 0.0 copy-start.13
  0.0 0.9 %copy-done.13 = f32[3,64,256]{2,1,0:T(8,128)S(1)} copy-done((f32[3,64,256]{2,1,0:T(8,128)S(1)}, f32[3,64,256]{2,1,0:T(8,128)}, u32[]{:S(2)}) %copy-start.13) | copy-done | bytes 196632
  0.9 0.8 copy-done.14
  1.8 9.9 %operator.1 = (bf16[256,256]{1,0:T(8,128)(2,1)S(1)}, f32[256,256]{1,0:T(8,128)S(1)}, f32[256,256]{1,0:T(8,128)S(1)}, f32[64,256]{1,0:T(8,128)S(1)}, f32[64,256]{...) custom-call(f32[3,64,256]{2,1,0:T(8,128)S(1)} %copy-done.13, f32[64,256]{1,0:T(8,128)S(1)} %copy-done.14), custom_call_target="tpu_custom_call" | custom-call | flops 20971520 | bytes 524288 | tf_op jit(solution)/shard_map/operator/pallas_call | solution.py:79
  11.6 0.0 copy-start.11
  11.7 0.7 copy-done.11
  12.3 0.0 copy-start.3
  12.3 0.0 copy-start.7
  12.3 0.0 copy-start.9
  12.4 0.0 copy-start.5
  12.4 0.0 copy-start
  12.4 1.5 %copy-done = bf16[64,48,256]{2,1,0:T(8,128)(2,1)S(1)} copy-done((bf16[64,48,256]{2,1,0:T(8,128)(2,1)S(1)}, bf16[64,48,256]{2,1,0:T(8,128)(2,1)}, u32[]{:S(2)}) %copy-start) | copy-done | bytes 1572888
  13.9 3.6 %ending.1 = (f32[48,256]{1,0:T(8,128)S(1)}, f32[48,256]{1,0:T(8,128)S(1)}) custom-call(bf16[2,32,48,256]{3,2,1,0:T(8,128)(2,1)S(1)} %bitcast.9, f32[2,32,256]{2,1,0:T(8,128)S(1)} %bitcast.12, f32[2,32,256]{2,1,0:T(8,128)S(1)} %bitcast.14, f32[2,32,256]{2,1,0:T(8,128)S(1)} %bitcast.16, f32[2,32,256]{2,1,0:T(8,128)S(1)} %bitcast.18, ...), custom_call_target="tpu_custom_call" | custom-call | flops 5505024 | bytes 1572864 | tf_op jit(solution)/shard_map/ending/pallas_call | solution.py:120
  17.4 0.1 collective-permute-start.3
  17.5 0.0 copy-done.3
  17.5 0.0 copy-done.7
  17.6 0.0 copy-done.9
  17.6 0.0 copy-done.5
  17.6 0.6 collective-permute-start
  18.1 0.0 copy-start.12
  18.2 0.6 collective-permute-done.3.their_end_ref
  18.8 0.3 collective-permute-done.their_op_ref
  19.1 0.2 convolution_convert_fusion
  19.3 0.7 collective-permute-start.2
  20.0 3.8 %collective-permute-start.1 = (bf16[256,256]{1,0:T(8,128)(2,1)S(1)}, bf16[256,256]{1,0:T(8,128)(2,1)S(1)}, u32[]{:S(2)}, u32[]{:S(2)}) collective-permute-start(bf16[256,256]{1,0:T(8,128)(2,1)S(1)} %convolution_convert_fusion), channel_id=1, source_target_pairs={{64,128},{96,160},{128,192},{160,224},{65,129},{97,161},{129,193},... | collective-permute-start | bytes 393224 | tf_op jit(solution)/shard_map/ppermute | solution.py:248
  23.8 0.2 fusion.2
  24.0 0.0 slice-start
  24.0 0.8 collective-permute-start.6
  24.8 1.4 %collective-permute-start.5 = (f32[48,256]{1,0:T(8,128)S(1)}, f32[48,256]{1,0:T(8,128)S(1)}, u32[]{:S(2)}, u32[]{:S(2)}) collective-permute-start(f32[48,256]{1,0:T(8,128)S(1)} %fusion.3), channel_id=1, source_target_pairs={{0,128},{32,160},{64,192},{96,224},{1,129},{33,161},{65,193},{97,2... | collective-permute-start | bytes 147464 | tf_op jit(solution)/shard_map/ppermute | solution.py:248
  26.2 1.9 %collective-permute-start.4 = (f32[48,256]{1,0:T(8,128)S(1)}, f32[48,256]{1,0:T(8,128)S(1)}, u32[]{:S(2)}, u32[]{:S(2)}) collective-permute-start(f32[48,256]{1,0:T(8,128)S(1)} %fusion.3), channel_id=1, source_target_pairs={{0,64},{32,96},{64,128},{96,160},{128,192},{160,224},{1,65},{33,97... | collective-permute-start | bytes 147464 | tf_op jit(solution)/shard_map/ppermute | solution.py:248
  28.2 0.0 collective-permute-done.6.chip_3_ref
  28.2 4.3 %collective-permute-done.5.chip_2_ref = f32[48,256]{1,0:T(8,128)S(1)} collective-permute-done((f32[48,256]{1,0:T(8,128)S(1)}, f32[48,256]{1,0:T(8,128)S(1)}, u32[]{:S(2)}, u32[]{:S(2)}) %collective-permute-start.5) | collective-permute-done | bytes 49184 | tf_op jit(solution)/shard_map/ppermute | solution.py:248
  32.5 0.6 collective-permute-done.4.chip_1_ref
  33.1 0.0 collective-permute-done.2.comp_2_ref
  33.1 0.0 collective-permute-done.1.comp_1_ref
  33.1 0.0 copy-done.1
  33.1 0.0 copy-done.2
  33.1 0.0 copy-done.4
  33.1 0.0 copy-done.6
  33.2 0.0 copy-done.8
  33.2 0.0 copy-done.10
  33.2 0.0 copy-done.12
  33.2 0.0 slice-start.1
  33.2 4.4 %gated.1 = bf16[2,32,48,256]{3,2,1,0:T(8,128)(2,1)S(1)} custom-call(s32[1]{0:T(128)} %bitcast.core_ref, bf16[256,256]{1,0:T(8,128)(2,1)S(1)} %collective-permute-done.1.comp_1_ref, bf16[256,256]{1,0:T(8,128)(2,1)S(1)} %collective-permute-done.2.comp_2_ref, f32[48,256]{1,0:T(8,128)S(1)} %collective-permute-done.4.chip_1_ref, ...), custom_call_target="tpu_custom_call" | custom-call | flops 9437184 | bytes 4718592 | tf_op jit(solution)/shard_map/gated/pallas_call | solution.py:181
  37.6 51.1 %all_to_all.5.gated_ref = bf16[32,2,48,256]{3,2,1,0:T(8,128)(2,1)S(1)} all-to-all(bf16[32,2,48,256]{3,2,1,0:T(8,128)(2,1)S(1)} %bitcast.8), channel_id=1, replica_groups=mesh['rows'=8,'chan'=32] {'chan'}, dimensions={0} | all-to-all | bytes 3145728 | tf_op jit(solution)/shard_map/all_to_all | solution.py:272
  88.7 0.0 slice-done
  88.7 0.0 slice-done.1
  88.7 3.5 %project.1 = bf16[2,1536,256]{2,1,0:T(8,128)(2,1)} custom-call(bf16[1536,1536]{1,0:T(8,128)(2,1)S(1)} %bitcast.21, bf16[32,2,48,256]{3,2,1,0:T(8,128)(2,1)S(1)} %all_to_all.5.gated_ref), custom_call_target="tpu_custom_call" | custom-call | flops 2415919104 | bytes 9437184 | tf_op jit(solution)/shard_map/project/pallas_call | solution.py:223
  (11 shorter events, 0.0 us)
Async XLA Ops:
  0.0 0.9 %copy-start.13 = (f32[3,64,256]{2,1,0:T(8,128)S(1)}, f32[3,64,256]{2,1,0:T(8,128)}, u32[]{:S(2)}) copy-start(f32[3,64,256]{2,1,0:T(8,128)} %mix_ref.1) | copy-start | bytes 589828
  0.9 0.8 copy-start.14
  11.6 0.7 copy-start.11
  12.3 5.2 %copy-start.3 = (f32[64,256]{1,0:T(8,128)}, f32[64,256]{1,0:T(8,128)S(1)}, u32[]{:S(2)}) copy-start(f32[64,256]{1,0:T(8,128)S(1)} %get-tuple-element.15) | copy-start | bytes 196612
  12.3 5.2 %copy-start.7 = (f32[64,256]{1,0:T(8,128)}, f32[64,256]{1,0:T(8,128)S(1)}, u32[]{:S(2)}) copy-start(f32[64,256]{1,0:T(8,128)S(1)} %get-tuple-element.17) | copy-start | bytes 196612
  12.3 5.2 %copy-start.9 = (f32[64,256]{1,0:T(8,128)}, f32[64,256]{1,0:T(8,128)S(1)}, u32[]{:S(2)}) copy-start(f32[64,256]{1,0:T(8,128)S(1)} %get-tuple-element.18) | copy-start | bytes 196612
  12.4 5.2 %copy-start.5 = (f32[64,256]{1,0:T(8,128)}, f32[64,256]{1,0:T(8,128)S(1)}, u32[]{:S(2)}) copy-start(f32[64,256]{1,0:T(8,128)S(1)} %get-tuple-element.16) | copy-start | bytes 196612
  12.4 1.5 %copy-start = (bf16[64,48,256]{2,1,0:T(8,128)(2,1)S(1)}, bf16[64,48,256]{2,1,0:T(8,128)(2,1)}, u32[]{:S(2)}) copy-start(bf16[64,48,256]{2,1,0:T(8,128)(2,1)} %param.5) | copy-start | bytes 4718596
  13.9 19.3 %copy-start.1 = (bf16[64,48,256]{2,1,0:T(8,128)(2,1)S(1)}, bf16[64,48,256]{2,1,0:T(8,128)(2,1)}, u32[]{:S(2)}) copy-start(bf16[64,48,256]{2,1,0:T(8,128)(2,1)} %param.5) | copy-start | bytes 4718596
  13.9 19.3 %copy-start.2 = (bf16[64,48,256]{2,1,0:T(8,128)(2,1)S(1)}, bf16[64,48,256]{2,1,0:T(8,128)(2,1)}, u32[]{:S(2)}) copy-start(bf16[64,48,256]{2,1,0:T(8,128)(2,1)} %param.8) | copy-start | bytes 4718596
  17.4 1.3 %collective-permute-start.3 = (f32[48,256]{1,0:T(8,128)S(1)}, f32[48,256]{1,0:T(8,128)S(1)}, u32[]{:S(2)}, u32[]{:S(2)}) collective-permute-start(f32[48,256]{1,0:T(8,128)S(1)} %get-tuple-element.20), channel_id=1, source_target_pairs={{0,32},{32,0},{64,96},{96,64},{128,160},{160,128},{192,224},{224,1... | collective-permute-start | bytes 147464 | tf_op jit(solution)/shard_map/ppermute | solution.py:251
  17.6 1.5 %collective-permute-start = (bf16[256,256]{1,0:T(8,128)(2,1)S(1)}, bf16[256,256]{1,0:T(8,128)(2,1)S(1)}, u32[]{:S(2)}, u32[]{:S(2)}) collective-permute-start(bf16[256,256]{1,0:T(8,128)(2,1)S(1)} %get-tuple-element.14), channel_id=1, source_target_pairs={{0,32},{32,0},{64,96},{96,64},{128,160},{160,128},{192,224},{224,1... | collective-permute-start | bytes 393224 | tf_op jit(solution)/shard_map/ppermute | solution.py:251
  18.1 15.0 %copy-start.4 = (f32[64,256]{1,0:T(8,128)S(1)}, f32[64,256]{1,0:T(8,128)}, u32[]{:S(2)}) copy-start(f32[64,256]{1,0:T(8,128)} %copy-done.3) | copy-start | bytes 196612
  18.1 15.0 %copy-start.6 = (f32[64,256]{1,0:T(8,128)S(1)}, f32[64,256]{1,0:T(8,128)}, u32[]{:S(2)}) copy-start(f32[64,256]{1,0:T(8,128)} %copy-done.5) | copy-start | bytes 196612
  18.1 15.0 %copy-start.8 = (f32[64,256]{1,0:T(8,128)S(1)}, f32[64,256]{1,0:T(8,128)}, u32[]{:S(2)}) copy-start(f32[64,256]{1,0:T(8,128)} %copy-done.7) | copy-start | bytes 196612
  18.1 15.0 %copy-start.10 = (f32[64,256]{1,0:T(8,128)S(1)}, f32[64,256]{1,0:T(8,128)}, u32[]{:S(2)}) copy-start(f32[64,256]{1,0:T(8,128)} %copy-done.9) | copy-start | bytes 196612
  18.1 15.0 %copy-start.12 = (f32[256,256]{1,0:T(8,128)S(1)}, f32[256,256]{1,0:T(8,128)}, u32[]{:S(2)}) copy-start(f32[256,256]{1,0:T(8,128)} %copy-done.11) | copy-start | bytes 786436
  19.3 13.8 %collective-permute-start.2 = (bf16[256,256]{1,0:T(8,128)(2,1)S(1)}, bf16[256,256]{1,0:T(8,128)(2,1)S(1)}, u32[]{:S(2)}, u32[]{:S(2)}) collective-permute-start(bf16[256,256]{1,0:T(8,128)(2,1)S(1)} %convolution_convert_fusion), channel_id=1, source_target_pairs={{64,192},{96,224},{65,193},{97,225},{66,194},{98,226},{67,195},{99... | collective-permute-start | bytes 393224 | tf_op jit(solution)/shard_map/ppermute | solution.py:248
  20.0 13.1 %collective-permute-start.1 = (bf16[256,256]{1,0:T(8,128)(2,1)S(1)}, bf16[256,256]{1,0:T(8,128)(2,1)S(1)}, u32[]{:S(2)}, u32[]{:S(2)}) collective-permute-start(bf16[256,256]{1,0:T(8,128)(2,1)S(1)} %convolution_convert_fusion), channel_id=1, source_target_pairs={{64,128},{96,160},{128,192},{160,224},{65,129},{97,161},{129,193},... | collective-permute-start | bytes 393224 | tf_op jit(solution)/shard_map/ppermute | solution.py:248
  24.0 64.8 %slice-start = ((s8[4718592]{0:T(1024)(128)(4,1)}), s8[4194304]{0:T(1024)(128)(4,1)S(1)}, s32[]{:S(2)}) async-start(s8[4718592]{0:T(1024)(128)(4,1)} %bitcast.20), calls=%async_computation.1 | async-start | bytes 8388608
  24.0 4.2 %collective-permute-start.6 = (f32[48,256]{1,0:T(8,128)S(1)}, f32[48,256]{1,0:T(8,128)S(1)}, u32[]{:S(2)}, u32[]{:S(2)}) collective-permute-start(f32[48,256]{1,0:T(8,128)S(1)} %fusion.3), channel_id=1, source_target_pairs={{0,192},{32,224},{1,193},{33,225},{2,194},{34,226},{3,195},{35,227... | collective-permute-start | bytes 147464 | tf_op jit(solution)/shard_map/ppermute | solution.py:248
  24.8 7.7 %collective-permute-start.5 = (f32[48,256]{1,0:T(8,128)S(1)}, f32[48,256]{1,0:T(8,128)S(1)}, u32[]{:S(2)}, u32[]{:S(2)}) collective-permute-start(f32[48,256]{1,0:T(8,128)S(1)} %fusion.3), channel_id=1, source_target_pairs={{0,128},{32,160},{64,192},{96,224},{1,129},{33,161},{65,193},{97,2... | collective-permute-start | bytes 147464 | tf_op jit(solution)/shard_map/ppermute | solution.py:248
  26.2 6.9 %collective-permute-start.4 = (f32[48,256]{1,0:T(8,128)S(1)}, f32[48,256]{1,0:T(8,128)S(1)}, u32[]{:S(2)}, u32[]{:S(2)}) collective-permute-start(f32[48,256]{1,0:T(8,128)S(1)} %fusion.3), channel_id=1, source_target_pairs={{0,64},{32,96},{64,128},{96,160},{128,192},{160,224},{1,65},{33,97... | collective-permute-start | bytes 147464 | tf_op jit(solution)/shard_map/ppermute | solution.py:248
  33.2 55.5 %slice-start.1 = ((s8[4718592]{0:T(1024)(128)(4,1)}), s8[524288]{0:T(1024)(128)(4,1)S(1)}, s32[]{:S(2)}) async-start(s8[4718592]{0:T(1024)(128)(4,1)} %bitcast.20), calls=%async_computation.2 | async-start | bytes 1048576
where the time goes:
time: 92.5 us; the launch traced here: 92.2 us
  blocking collectives  51.1 us (55%)
  Pallas kernels  21.3 us (23%)
  starting transfers between devices  9.27 us (10%)
  waiting for transfers between devices  5.88 us (6%)
  local copies, waits for them, and re-layouts  4.02 us (4%)
    all_to_all x1, blocking collectives, shards(): lax.all_to_all(mixed, 'chan', split_axis=0, concat_axis=0, tiled=True)  51.1 us
    pallas_call x1, Pallas kernels, operator_of(): pl.pallas_call(operator_kernel, out_shape=(jax.ShapeDtypeStruct((width, w...  9.86 us
    ppermute x5, starting transfers between devices, chips_back(): lax.ppermute(value, 'rows', [(i, i + 2 * shift) for i in range(2 * chip,...  8.62 us
    ppermute x5, waiting for transfers between devices, chips_back(): lax.ppermute(value, 'rows', [(i, i + 2 * shift) for i in range(2 * chip,...  4.94 us
    pallas_call x1, Pallas kernels, gated(): pl.pallas_call(gated_kernel, grid_spec=pltpu.PrefetchScalarGridSpec(num_s...  4.37 us
    unnamed x34, local copies, waits for them, and re-layouts  4.02 us
    pallas_call x1, Pallas kernels, ending(): pl.pallas_call(ending_kernel, grid=(rows // STEP_ROWS,), in_specs=[pl.Blo...  3.56 us
    pallas_call x1, Pallas kernels, project(): pl.pallas_call(project_kernel, in_specs=[pl.BlockSpec(memory_space=pltpu....  3.47 us
  transfers between devices with their start and end apart: 7, of which 4 were waited for; matrix products, arithmetic and copies ran while one was open for 0% of the time, Pallas kernels for 0%

commit v1 on v0

--- a/solution.py
+++ b/solution.py
@@ -6,11 +6,11 @@
 from jax.sharding import PartitionSpec as P
 
 STEP_ROWS = 8
-HALF = 128
-REACH = 32
+BLOCK = 8
+SUBLANES = 8
+LANES = 128
 TILES = 4
 VMEM_LIMIT = 16 * 1024 * 1024
-HIGHEST = lax.Precision.HIGHEST
 
 
 def stencil(state, left_w, mid_w, right_w):
@@ -20,66 +20,103 @@
     return left_w * before_col + mid_w * state + right_w * after_col
 
 
-def diagonal(first, count, left, width):
-    source = lax.broadcasted_iota(jnp.int32, (count, width), 0) + first
-    column = lax.broadcasted_iota(jnp.int32, (count, width), 1) + left
-    return jnp.where(source == column, 1.0, 0.0).astype(jnp.float32)
+def split(value):
+    high = value.astype(jnp.bfloat16)
+    return high, (value - high.astype(jnp.float32)).astype(jnp.bfloat16)
+
+
+def product(left, right):
+    (left_high, left_low), (right_high, right_low) = left, right
+    out = jnp.dot(left_high, right_high, preferred_element_type=jnp.float32)
+    out = out + jnp.dot(left_high, right_low, preferred_element_type=jnp.float32)
+    return out + jnp.dot(left_low, right_high, preferred_element_type=jnp.float32)
 
 
 def operator_kernel(
-    mix_ref, decay_ref, op_ref, early_ref, late_ref, left_ref, mid_ref, right_ref, in_ref, left_cut_ref, right_cut_ref
+    mix_ref, decay_ref, op_ref, early_ref, late_ref, left_ref, mid_ref, right_ref, in_ref,
+    side_ref, diag_ref, dense_ref,
 ):
     rows, width = decay_ref.shape
     decay = decay_ref[...]
     retain = 1.0 - decay
-    column = lax.broadcasted_iota(jnp.int32, (rows, width), 1)
-    left_w = retain * mix_ref[0]
-    right_w = retain * mix_ref[2]
-    left_ref[...] = left_w
-    mid_ref[...] = retain * mix_ref[1]
-    right_ref[...] = right_w
+    for side, ref in enumerate((left_ref, mid_ref, right_ref)):
+        value = retain * mix_ref[side]
+        ref[...] = value
+        for part in range(width // LANES):
+            side_ref[side, part] = value[:, part * LANES : (part + 1) * LANES]
     in_ref[...] = jnp.sqrt(decay)
-    left_cut_ref[...] = jnp.where(column == HALF, 0.0, left_w)
-    right_cut_ref[...] = jnp.where(column == HALF - 1, 0.0, right_w)
-
-    inner = HALF - REACH
-    outs = (early_ref, late_ref)
-    for out in outs:
-        out[0:inner, HALF:width] = jnp.zeros((inner, width - HALF), jnp.float32)
-        out[width - inner : width, 0:HALF] = jnp.zeros((inner, HALF), jnp.float32)
-
-    def sweep(first, count, left, right, lefts, rights):
-        lanes = slice(left, right)
-
-        def step(i, states):
-            news = []
-            for half in range(2):
-                row = pl.ds(i + half * REACH, 1)
-                weights = [ref[row, :][:, lanes] for ref in (lefts, mid_ref, rights)]
-                news.append(stencil(states[half], *weights))
-            return tuple(news)
-
-        start = diagonal(first, count, left, right - left)
-        finals = lax.fori_loop(0, REACH, step, (start, start), unroll=4)
-        for out, final in zip(outs, finals):
-            out[first : first + count, lanes] = final
-
-    sweep(0, inner, 0, HALF, left_ref, right_cut_ref)
-    sweep(width - inner, inner, HALF, width, left_cut_ref, right_ref)
-    sweep(inner, 2 * REACH, 0, width, left_ref, right_ref)
-    op_ref[...] = jnp.dot(
-        early_ref[...], late_ref[...], precision=HIGHEST, preferred_element_type=jnp.float32
-    ).astype(op_ref.dtype)
+
+    blocks = rows // BLOCK
+
+    def weights(j):
+        row = pl.ds(j, blocks, stride=BLOCK)
+        return [
+            jnp.concatenate([side_ref[side, part, row, :] for part in range(width // LANES)], axis=1)
+            for side in range(3)
+        ]
+
+    left_w, mid_w, right_w = weights(0)
+    diagonals = {-1: left_w, 0: mid_w, 1: right_w}
+    for j in range(1, BLOCK):
+        left_w, mid_w, right_w = weights(j)
+        news = {}
+        for d, values in diagonals.items():
+            terms = (
+                (d - 1, left_w * pltpu.roll(values, 1, 1)),
+                (d, mid_w * values),
+                (d + 1, right_w * pltpu.roll(values, width - 1, 1)),
+            )
+            for to, term in terms:
+                news[to] = news[to] + term if to in news else term
+        diagonals = news
+    for d, values in diagonals.items():
+        diag_ref[d + BLOCK] = values
+
+    lead = lax.broadcasted_iota(jnp.int32, (SUBLANES, LANES), 1) - lax.broadcasted_iota(
+        jnp.int32, (SUBLANES, LANES), 0
+    )
+    for left in range(0, width, LANES):
+        lanes = slice(left, left + LANES)
+        low = max(0, left - SUBLANES)
+        high = min(width, left + LANES + SUBLANES)
+        for b in range(blocks):
+            if low > 0:
+                dense_ref[b, 0:low, lanes] = jnp.zeros((low, LANES), jnp.float32)
+            if high < width:
+                dense_ref[b, high:width, lanes] = jnp.zeros((width - high, LANES), jnp.float32)
+        for top in range(low, high, SUBLANES):
+            tiles = [jnp.zeros((SUBLANES, LANES), jnp.float32)] * blocks
+            for d in range(-BLOCK, BLOCK + 1):
+                offset = top - d - left
+                if -SUBLANES < offset < LANES:
+                    here = lead == offset
+                    for b in range(blocks):
+                        row = jnp.broadcast_to(diag_ref[d + BLOCK, b : b + 1, lanes], (SUBLANES, LANES))
+                        tiles[b] = jnp.where(here, row, tiles[b])
+            for b in range(blocks):
+                dense_ref[b, top : top + SUBLANES, lanes] = tiles[b]
+
+    pairs = [split(product(split(dense_ref[b]), split(dense_ref[b + 1]))) for b in range(0, blocks, 2)]
+    early = split(product(pairs[0], pairs[1]))
+    late = split(product(pairs[2], pairs[3]))
+    for out, value in ((early_ref, early), (late_ref, late)):
+        out[0] = value[0]
+        out[1] = value[1]
+    op_ref[...] = product(early, late).astype(op_ref.dtype)
 
 
 def operator_of(mixing, decay_rate):
     _, rows, width = mixing.shape
-    square = jax.ShapeDtypeStruct((width, width), jnp.float32)
+    halves = jax.ShapeDtypeStruct((2, width, width), jnp.bfloat16)
     coef = jax.ShapeDtypeStruct((rows, width), jnp.float32)
     return pl.pallas_call(
         operator_kernel,
-        out_shape=(jax.ShapeDtypeStruct((width, width), jnp.bfloat16), square, square, coef, coef, coef, coef),
-        scratch_shapes=[pltpu.VMEM((rows, width), jnp.float32)] * 2,
+        out_shape=(jax.ShapeDtypeStruct((width, width), jnp.bfloat16), halves, halves, coef, coef, coef, coef),
+        scratch_shapes=[
+            pltpu.VMEM((3, width // LANES, rows, LANES), jnp.float32),
+            pltpu.VMEM((2 * BLOCK + 1, rows // BLOCK, width), jnp.float32),
+            pltpu.VMEM((rows // BLOCK, width, width), jnp.float32),
+        ],
         cost_estimate=pl.CostEstimate(
             flops=5 * rows * width * width, bytes_accessed=8 * rows * width * 4, transcendentals=0
         ),
@@ -107,9 +144,7 @@
     @pl.when(pl.program_id(0) == pl.num_programs(0) - 1)
     def _():
         early_end_ref[...] = states[0]
-        end_ref[...] = states[1] + jnp.dot(
-            states[0], late_ref[...], precision=HIGHEST, preferred_element_type=jnp.float32
-        )
+        end_ref[...] = states[1] + product(split(states[0]), (late_ref[0], late_ref[1]))
 
 
 def ending(features, coefs, late):
@@ -122,7 +157,7 @@
         grid=(rows // STEP_ROWS,),
         in_specs=[pl.BlockSpec((2, STEP_ROWS, channels, width), lambda i: (0, i, 0, 0))]
         + [coef_spec] * 4
-        + [pl.BlockSpec((width, width), lambda i: (0, 0))],
+        + [pl.BlockSpec((2, width, width), lambda i: (0, 0, 0))],
         out_specs=(state_spec, state_spec),
         out_shape=(state, state),
         scratch_shapes=[pltpu.VMEM((2, channels, width), jnp.float32)],
@@ -135,26 +170,21 @@
 
 
 def applied(state, operator):
-    high = state.astype(jnp.bfloat16)
-    low = (state - high.astype(jnp.float32)).astype(jnp.bfloat16)
-    both = jnp.dot(jnp.concatenate([high, low]), operator, preferred_element_type=jnp.float32)
+    both = jnp.dot(jnp.concatenate(split(state)), operator, preferred_element_type=jnp.float32)
     return both[: state.shape[0]] + both[state.shape[0] :]
 
 
 def gated_kernel(
-    core_ref, comp_1_ref, comp_2_ref, chip_1_ref, chip_2_ref, chip_3_ref, their_op_ref, their_end_ref,
-    early_ref, early_end_ref, feat_ref, gate_ref, left_ref, mid_ref, right_ref, in_ref, out_ref, state_ref,
+    core_ref, hop_1_ref, hop_2_ref, hop_3_ref, their_op_ref, their_end_ref, early_ref, early_end_ref,
+    feat_ref, gate_ref, left_ref, mid_ref, right_ref, in_ref, out_ref, state_ref,
 ):
     @pl.when(pl.program_id(0) == 0)
     def _():
-        incoming = applied(chip_3_ref[...], comp_2_ref[...]) + chip_2_ref[...]
-        incoming = applied(incoming, comp_1_ref[...]) + chip_1_ref[...]
+        incoming = hop_1_ref[...] + hop_2_ref[...] + hop_3_ref[...]
         later = applied(incoming, their_op_ref[...]) + their_end_ref[...]
         incoming = jnp.where(core_ref[0] == 0, incoming, later)
         state_ref[0] = incoming
-        state_ref[1] = early_end_ref[...] + jnp.dot(
-            incoming, early_ref[...], precision=HIGHEST, preferred_element_type=jnp.float32
-        )
+        state_ref[1] = early_end_ref[...] + product(split(incoming), (early_ref[0], early_ref[1]))
 
     states = [state_ref[0], state_ref[1]]
     for j in range(feat_ref.shape[1]):
@@ -244,8 +274,8 @@
     core = lax.axis_index("rows") % 2
     first = core == 0
 
-    def chips_back(value, shift, chip):
-        return lax.ppermute(value, "rows", [(i, i + 2 * shift) for i in range(2 * chip, slabs - 2 * shift)])
+    def hop(value, chip):
+        return lax.ppermute(value, "rows", [(2 * chip + c, 2 * chip + 2 + c) for c in range(2)])
 
     def swapped(value):
         return lax.ppermute(value, "rows", [(i, i ^ 1) for i in range(slabs)])
@@ -256,17 +286,17 @@
     operator, early, late, *coefs = operator_of(mixing, decay_rate)
     coefs = [c.reshape(2, rows // 2, width) for c in coefs]
     their_op = swapped(operator)
+    early_end, end = ending(features, coefs, late)
+    their_end = swapped(end)
     op_0, op_1 = in_order(operator, their_op)
     composite = jnp.dot(op_0, op_1, preferred_element_type=jnp.float32).astype(jnp.bfloat16)
-    comp_2 = chips_back(composite, 2, 1)
-    comp_1 = chips_back(composite, 1, 1)
-    early_end, end = ending(features, coefs, late)
-    their_end = swapped(end)
     end_0, end_1 = in_order(end, their_end)
     chip_end = applied(end_0, op_1) + end_1
-    chip_3, chip_2, chip_1 = [chips_back(chip_end, shift, 0) for shift in (3, 2, 1)]
-
-    starts = (comp_1, comp_2, chip_1, chip_2, chip_3, their_op, their_end, early, early_end)
+    hops = [hop(chip_end, 0)]
+    for chip in range(1, slabs // 2 - 1):
+        hops.append(hop(applied(hops[-1], composite) + chip_end, chip))
+
+    starts = (*hops, their_op, their_end, early, early_end)
     mixed = gated(core.astype(jnp.int32).reshape(1), starts, features, gate_input, coefs)
     mixed = mixed.reshape(peers, rows // peers, channels, width)
     return project(out_weight, lax.all_to_all(mixed, "chan", split_axis=0, concat_axis=0, tiled=True))

time: 92.5 us -> 83.2 us (0.90)
  the two profiles are of different devices: /device:TPU:48 before, /device:TPU:56 now
where the time goes in v1:
time: 83.2 us; the launch traced here: 82.9 us
  blocking collectives  48.8 us (59%)
  Pallas kernels  13.8 us (17%)
  waiting for transfers between devices  11.9 us (14%)
  local copies, waits for them, and re-layouts  4.03 us (5%)
  starting transfers between devices  3.46 us (4%)
    all_to_all x1, blocking collectives, shards(): lax.all_to_all(mixed, 'chan', split_axis=0, concat_axis=0, tiled=True)  48.8 us
    ppermute x3, waiting for transfers between devices, hop(): lax.ppermute(value, 'rows', [(2 * chip + c, 2 * chip + 2 + c) for c in ra...  11 us
    unnamed x34, local copies, waits for them, and re-layouts  4.03 us
    pallas_call x1, Pallas kernels, gated(): pl.pallas_call(gated_kernel, grid_spec=pltpu.PrefetchScalarGridSpec(num_s...  4.01 us
    pallas_call x1, Pallas kernels, ending(): pl.pallas_call(ending_kernel, grid=(rows // STEP_ROWS,), in_specs=[pl.Blo...  3.49 us
    pallas_call x1, Pallas kernels, project(): pl.pallas_call(project_kernel, in_specs=[pl.BlockSpec(memory_space=pltpu....  3.47 us
    ppermute x3, starting transfers between devices, hop(): lax.ppermute(value, 'rows', [(2 * chip + c, 2 * chip + 2 + c) for c in ra...  2.88 us
    pallas_call x1, Pallas kernels, operator_of(): pl.pallas_call(operator_kernel, out_shape=(jax.ShapeDtypeStruct((width, w...  2.83 us
  transfers between devices with their start and end apart: 5, of which 3 were waited for; matrix products, arithmetic and copies ran while one was open for 0% of the time, Pallas kernels for 0%

profile of v1, /device:TPU:56, one launch (start us, length us, event | category | flops | bytes accessed | tf_op | source)
XLA Modules:
  0.0 82.9 jit_solution(3849358486081960281)
XLA Ops:
  0.0 0.0 copy-start.13
  0.0 0.9 %copy-done.13 = f32[3,64,256]{2,1,0:T(8,128)S(1)} copy-done((f32[3,64,256]{2,1,0:T(8,128)S(1)}, f32[3,64,256]{2,1,0:T(8,128)}, u32[]{:S(2)}) %copy-start.13) | copy-done | bytes 196632
  0.9 0.0 copy-start.14
  0.9 0.8 %copy-done.14 = f32[64,256]{1,0:T(8,128)S(1)} copy-done((f32[64,256]{1,0:T(8,128)S(1)}, f32[64,256]{1,0:T(8,128)}, u32[]{:S(2)}) %copy-start.14) | copy-done | bytes 65560
  1.8 2.8 %operator.1 = (bf16[256,256]{1,0:T(8,128)(2,1)S(1)}, bf16[2,256,256]{2,1,0:T(8,128)(2,1)S(1)}, bf16[2,256,256]{2,1,0:T(8,128)(2,1)S(1)}, f32[64,256]{1,0:T(8,128...) custom-call(f32[3,64,256]{2,1,0:T(8,128)S(1)} %copy-done.13, f32[64,256]{1,0:T(8,128)S(1)} %copy-done.14), custom_call_target="tpu_custom_call" | custom-call | flops 20971520 | bytes 524288 | tf_op jit(solution)/shard_map/operator/pallas_call | solution.py:112
  4.6 0.0 copy-start.11
  4.6 0.7 copy-done.11
  5.3 0.0 copy-start.3
  5.3 0.0 copy-start.5
  5.3 0.0 copy-start
  5.3 1.5 %copy-done = bf16[64,48,256]{2,1,0:T(8,128)(2,1)S(1)} copy-done((bf16[64,48,256]{2,1,0:T(8,128)(2,1)S(1)}, bf16[64,48,256]{2,1,0:T(8,128)(2,1)}, u32[]{:S(2)}) %copy-start) | copy-done | bytes 1572888
  6.8 3.5 %ending.1 = (f32[48,256]{1,0:T(8,128)S(1)}, f32[48,256]{1,0:T(8,128)S(1)}) custom-call(bf16[2,32,48,256]{3,2,1,0:T(8,128)(2,1)S(1)} %bitcast.11, f32[2,32,256]{2,1,0:T(8,128)S(1)} %bitcast.14, f32[2,32,256]{2,1,0:T(8,128)S(1)} %bitcast.16, f32[2,32,256]{2,1,0:T(8,128)S(1)} %bitcast.18, f32[2,32,256]{2,1,0:T(8,128)S(1)} %bitcast.20, ...), custom_call_target="tpu_custom_call" | custom-call | flops 5505024 | bytes 1572864 | tf_op jit(solution)/shard_map/ending/pallas_call | solution.py:155
  10.3 0.0 copy-start.1
  10.3 0.1 collective-permute-start
  10.4 0.0 copy-done.3
  10.5 0.0 copy-done.5
  10.5 0.5 collective-permute-start.1
  10.9 0.0 copy-done.7
  10.9 0.0 copy-done.9
  11.0 0.0 copy-start.8
  11.0 0.0 copy-start.10
  11.0 0.0 copy-start.12
  11.0 0.7 collective-permute-done.their_end_ref
  11.7 0.2 collective-permute-done.1.their_op_ref
  11.9 0.1 fusion.2
  12.1 0.7 collective-permute-start.2
  12.8 0.2 convolution_convert_fusion
  13.0 0.0 collective-permute-done.2.hop_1_ref
  13.0 0.1 fusion.9
  13.2 0.7 collective-permute-start.3
  13.9 0.0 collective-permute-done.3.hop_2_ref
  13.9 0.1 fusion.13
  14.0 0.0 slice-start
  14.1 1.6 %collective-permute-start.4 = (f32[48,256]{1,0:T(8,128)S(1)}, f32[48,256]{1,0:T(8,128)S(1)}, u32[]{:S(2)}, u32[]{:S(2)}) collective-permute-start(f32[48,256]{1,0:T(8,128)S(1)} %fusion.3), channel_id=1, source_target_pairs={{128,192},{160,224},{129,193},{161,225},{130,194},{162,226},{131,1... | collective-permute-start | bytes 147464 | tf_op jit(solution)/shard_map/ppermute | solution.py:278
  15.6 11.0 %collective-permute-done.4.hop_3_ref = f32[48,256]{1,0:T(8,128)S(1)} collective-permute-done((f32[48,256]{1,0:T(8,128)S(1)}, f32[48,256]{1,0:T(8,128)S(1)}, u32[]{:S(2)}, u32[]{:S(2)}) %collective-permute-start.4) | collective-permute-done | bytes 49184 | tf_op jit(solution)/shard_map/ppermute | solution.py:278
  26.6 0.0 copy-done.2
  26.6 0.0 copy-done.1
  26.6 0.0 copy-done.4
  26.6 0.0 copy-done.6
  26.6 0.0 copy-done.8
  26.6 0.0 copy-done.10
  26.6 0.0 copy-done.12
  26.7 0.0 slice-start.1
  26.7 4.0 %gated.1 = bf16[2,32,48,256]{3,2,1,0:T(8,128)(2,1)S(1)} custom-call(s32[1]{0:T(128)} %bitcast.core_ref, f32[48,256]{1,0:T(8,128)S(1)} %collective-permute-done.2.hop_1_ref, f32[48,256]{1,0:T(8,128)S(1)} %collective-permute-done.3.hop_2_ref, f32[48,256]{1,0:T(8,128)S(1)} %collective-permute-done.4.hop_3_ref, ...), custom_call_target="tpu_custom_call" | custom-call | flops 9437184 | bytes 4718592 | tf_op jit(solution)/shard_map/gated/pallas_call | solution.py:211
  30.7 48.8 %all_to_all.5.gated_ref = bf16[32,2,48,256]{3,2,1,0:T(8,128)(2,1)S(1)} all-to-all(bf16[32,2,48,256]{3,2,1,0:T(8,128)(2,1)S(1)} %bitcast.10), channel_id=1, replica_groups=mesh['rows'=8,'chan'=32] {'chan'}, dimensions={0} | all-to-all | bytes 3145728 | tf_op jit(solution)/shard_map/all_to_all | solution.py:302
  79.5 0.0 slice-done
  79.5 0.0 slice-done.1
  79.5 3.5 %project.1 = bf16[2,1536,256]{2,1,0:T(8,128)(2,1)} custom-call(bf16[1536,1536]{1,0:T(8,128)(2,1)S(1)} %bitcast.23, bf16[32,2,48,256]{3,2,1,0:T(8,128)(2,1)S(1)} %all_to_all.5.gated_ref), custom_call_target="tpu_custom_call" | custom-call | flops 2415919104 | bytes 9437184 | tf_op jit(solution)/shard_map/project/pallas_call | solution.py:253
  (13 shorter events, 0.1 us)
Async XLA Ops:
  0.0 0.9 %copy-start.13 = (f32[3,64,256]{2,1,0:T(8,128)S(1)}, f32[3,64,256]{2,1,0:T(8,128)}, u32[]{:S(2)}) copy-start(f32[3,64,256]{2,1,0:T(8,128)} %mix_ref.1) | copy-start | bytes 589828
  0.9 0.8 %copy-start.14 = (f32[64,256]{1,0:T(8,128)S(1)}, f32[64,256]{1,0:T(8,128)}, u32[]{:S(2)}) copy-start(f32[64,256]{1,0:T(8,128)} %decay_ref.1) | copy-start | bytes 196612
  4.6 0.7 copy-start.11
  5.3 5.1 %copy-start.3 = (f32[64,256]{1,0:T(8,128)}, f32[64,256]{1,0:T(8,128)S(1)}, u32[]{:S(2)}) copy-start(f32[64,256]{1,0:T(8,128)S(1)} %get-tuple-element.14) | copy-start | bytes 196612
  5.3 5.1 %copy-start.5 = (f32[64,256]{1,0:T(8,128)}, f32[64,256]{1,0:T(8,128)S(1)}, u32[]{:S(2)}) copy-start(f32[64,256]{1,0:T(8,128)S(1)} %get-tuple-element.15) | copy-start | bytes 196612
  5.3 5.6 %copy-start.7 = (f32[64,256]{1,0:T(8,128)}, f32[64,256]{1,0:T(8,128)S(1)}, u32[]{:S(2)}) copy-start(f32[64,256]{1,0:T(8,128)S(1)} %get-tuple-element.16) | copy-start | bytes 196612
  5.3 5.6 %copy-start.9 = (f32[64,256]{1,0:T(8,128)}, f32[64,256]{1,0:T(8,128)S(1)}, u32[]{:S(2)}) copy-start(f32[64,256]{1,0:T(8,128)S(1)} %get-tuple-element.17) | copy-start | bytes 196612
  5.3 1.5 %copy-start = (bf16[64,48,256]{2,1,0:T(8,128)(2,1)S(1)}, bf16[64,48,256]{2,1,0:T(8,128)(2,1)}, u32[]{:S(2)}) copy-start(bf16[64,48,256]{2,1,0:T(8,128)(2,1)} %param.5) | copy-start | bytes 4718596
  6.8 19.8 %copy-start.2 = (bf16[64,48,256]{2,1,0:T(8,128)(2,1)S(1)}, bf16[64,48,256]{2,1,0:T(8,128)(2,1)}, u32[]{:S(2)}) copy-start(bf16[64,48,256]{2,1,0:T(8,128)(2,1)} %param.8) | copy-start | bytes 4718596
  10.3 16.3 %copy-start.1 = (bf16[64,48,256]{2,1,0:T(8,128)(2,1)S(1)}, bf16[64,48,256]{2,1,0:T(8,128)(2,1)}, u32[]{:S(2)}) copy-start(bf16[64,48,256]{2,1,0:T(8,128)(2,1)} %param.5) | copy-start | bytes 4718596
  10.3 1.3 %collective-permute-start = (f32[48,256]{1,0:T(8,128)S(1)}, f32[48,256]{1,0:T(8,128)S(1)}, u32[]{:S(2)}, u32[]{:S(2)}) collective-permute-start(f32[48,256]{1,0:T(8,128)S(1)} %get-tuple-element.19), channel_id=1, source_target_pairs={{0,32},{32,0},{64,96},{96,64},{128,160},{160,128},{192,224},{224,1... | collective-permute-start | bytes 147464 | tf_op jit(solution)/shard_map/ppermute | solution.py:281
  10.5 1.5 %collective-permute-start.1 = (bf16[256,256]{1,0:T(8,128)(2,1)S(1)}, bf16[256,256]{1,0:T(8,128)(2,1)S(1)}, u32[]{:S(2)}, u32[]{:S(2)}) collective-permute-start(bf16[256,256]{1,0:T(8,128)(2,1)S(1)} %get-tuple-element.20), channel_id=1, source_target_pairs={{0,32},{32,0},{64,96},{96,64},{128,160},{160,128},{192,224},{224,1... | collective-permute-start | bytes 393224 | tf_op jit(solution)/shard_map/ppermute | solution.py:281
  11.0 15.7 %copy-start.4 = (f32[64,256]{1,0:T(8,128)S(1)}, f32[64,256]{1,0:T(8,128)}, u32[]{:S(2)}) copy-start(f32[64,256]{1,0:T(8,128)} %copy-done.3) | copy-start | bytes 196612
  11.0 15.7 %copy-start.6 = (f32[64,256]{1,0:T(8,128)S(1)}, f32[64,256]{1,0:T(8,128)}, u32[]{:S(2)}) copy-start(f32[64,256]{1,0:T(8,128)} %copy-done.5) | copy-start | bytes 196612
  11.0 15.7 %copy-start.8 = (f32[64,256]{1,0:T(8,128)S(1)}, f32[64,256]{1,0:T(8,128)}, u32[]{:S(2)}) copy-start(f32[64,256]{1,0:T(8,128)} %copy-done.7) | copy-start | bytes 196612
  11.0 15.7 %copy-start.10 = (f32[64,256]{1,0:T(8,128)S(1)}, f32[64,256]{1,0:T(8,128)}, u32[]{:S(2)}) copy-start(f32[64,256]{1,0:T(8,128)} %copy-done.9) | copy-start | bytes 196612
  11.0 15.7 %copy-start.12 = (bf16[2,256,256]{2,1,0:T(8,128)(2,1)S(1)}, bf16[2,256,256]{2,1,0:T(8,128)(2,1)}, u32[]{:S(2)}) copy-start(bf16[2,256,256]{2,1,0:T(8,128)(2,1)} %copy-done.11) | copy-start | bytes 786436
  12.1 0.9 %collective-permute-start.2 = (f32[48,256]{1,0:T(8,128)S(1)}, f32[48,256]{1,0:T(8,128)S(1)}, u32[]{:S(2)}, u32[]{:S(2)}) collective-permute-start(f32[48,256]{1,0:T(8,128)S(1)} %fusion.5), channel_id=1, source_target_pairs={{0,64},{32,96},{1,65},{33,97},{2,66},{34,98},{3,67},{35,99},{4,68}... | collective-permute-start | bytes 147464 | tf_op jit(solution)/shard_map/ppermute | solution.py:278
  13.2 0.7 collective-permute-start.3
  14.0 65.4 %slice-start = ((s8[4718592]{0:T(1024)(128)(4,1)}), s8[4194304]{0:T(1024)(128)(4,1)S(1)}, s32[]{:S(2)}) async-start(s8[4718592]{0:T(1024)(128)(4,1)} %bitcast.22), calls=%async_computation.1 | async-start | bytes 8388608
  14.1 12.5 %collective-permute-start.4 = (f32[48,256]{1,0:T(8,128)S(1)}, f32[48,256]{1,0:T(8,128)S(1)}, u32[]{:S(2)}, u32[]{:S(2)}) collective-permute-start(f32[48,256]{1,0:T(8,128)S(1)} %fusion.3), channel_id=1, source_target_pairs={{128,192},{160,224},{129,193},{161,225},{130,194},{162,226},{131,1... | collective-permute-start | bytes 147464 | tf_op jit(solution)/shard_map/ppermute | solution.py:278
  26.7 52.8 %slice-start.1 = ((s8[4718592]{0:T(1024)(128)(4,1)}), s8[524288]{0:T(1024)(128)(4,1)S(1)}, s32[]{:S(2)}) async-start(s8[4718592]{0:T(1024)(128)(4,1)} %bitcast.22), calls=%async_computation.2 | async-start | bytes 1048576

commit v2 on v1

v2 whole, which is shorter than its diff:
```python
import jax
import jax.numpy as jnp
from jax import lax
from jax.experimental import pallas as pl
from jax.experimental.pallas import tpu as pltpu
from jax.sharding import PartitionSpec as P

UNROLL = 8
BLOCK = 8
SUBLANES = 8
LANES = 128
TILES = 4
MIB = 1024 * 1024
SUMMARY_MIB = 62


def stencil(state, left_w, mid_w, right_w):
    width = state.shape[1]
    before_col = pltpu.roll(state, 1, 1)
    after_col = pltpu.roll(state, width - 1, 1)
    return left_w * before_col + mid_w * state + right_w * after_col


def split(value):
    high = value.astype(jnp.bfloat16)
    return high, (value - high.astype(jnp.float32)).astype(jnp.bfloat16)


def product(left, right):
    (left_high, left_low), (right_high, right_low) = left, right
    out = jnp.dot(left_high, right_high, preferred_element_type=jnp.float32)
    out = out + jnp.dot(left_high, right_low, preferred_element_type=jnp.float32)
    return out + jnp.dot(left_low, right_high, preferred_element_type=jnp.float32)


def sweep(states, feat_ref, keep_ref, rows, take=None):
    def step(i, states):
        news = []
        for half in range(2):
            left_w, mid_w, right_w, in_w = [
                keep_ref[pl.ds(i + half * rows + k * 2 * rows, 1), :] for k in range(4)
            ]
            push = in_w * feat_ref[i + half * rows].astype(jnp.float32)
            news.append(stencil(states[half], left_w, mid_w, right_w) + push)
            if take is not None:
                take(i + half * rows, news[half])
        return tuple(news)

    return lax.fori_loop(0, rows, step, states, unroll=UNROLL)


def summary_kernel(
    mix_hbm, decay_hbm, feat_hbm, pack_ref, keep_ref,
    mix_ref, decay_ref, feat_ref, sem_ref, side_ref, diag_ref, dense_ref,
):
    copies = [
        pltpu.make_async_copy(source, target, sem_ref.at[k])
        for k, (source, target) in enumerate(
            ((mix_hbm, mix_ref), (decay_hbm, decay_ref), (feat_hbm, feat_ref))
        )
    ]
    for copy in copies:
        copy.start()
    copies[0].wait()
    copies[1].wait()
    rows, width = decay_ref.shape
    decay = decay_ref[...]
    retain = 1.0 - decay
    for side in range(3):
        value = retain * mix_ref[side]
        keep_ref[side * rows : (side + 1) * rows] = value
        for part in range(width // LANES):
            side_ref[side, part] = value[:, part * LANES : (part + 1) * LANES]
    keep_ref[3 * rows : 4 * rows] = jnp.sqrt(decay)

    blocks = rows // BLOCK

    def weights(j):
        row = pl.ds(j, blocks, stride=BLOCK)
        return [
            jnp.concatenate([side_ref[side, part, row, :] for part in range(width // LANES)], axis=1)
            for side in range(3)
        ]

    left_w, mid_w, right_w = weights(0)
    diagonals = {-1: left_w, 0: mid_w, 1: right_w}
    for j in range(1, BLOCK):
        left_w, mid_w, right_w = weights(j)
        news = {}
        for d, values in diagonals.items():
            terms = (
                (d - 1, left_w * pltpu.roll(values, 1, 1)),
                (d, mid_w * values),
                (d + 1, right_w * pltpu.roll(values, width - 1, 1)),
            )
            for to, term in terms:
                news[to] = news[to] + term if to in news else term
        diagonals = news
    for d, values in diagonals.items():
        diag_ref[d + BLOCK] = values

    lead = lax.broadcasted_iota(jnp.int32, (SUBLANES, LANES), 1) - lax.broadcasted_iota(
        jnp.int32, (SUBLANES, LANES), 0
    )
    for left in range(0, width, LANES):
        lanes = slice(left, left + LANES)
        low = max(0, left - SUBLANES)
        high = min(width, left + LANES + SUBLANES)
        for b in range(blocks):
            if low > 0:
                dense_ref[b, 0:low, lanes] = jnp.zeros((low, LANES), jnp.float32)
            if high < width:
                dense_ref[b, high:width, lanes] = jnp.zeros((width - high, LANES), jnp.float32)
        for top in range(low, high, SUBLANES):
            tiles = [jnp.zeros((SUBLANES, LANES), jnp.float32)] * blocks
            for d in range(-BLOCK, BLOCK + 1):
                offset = top - d - left
                if -SUBLANES < offset < LANES:
                    here = lead == offset
                    for b in range(blocks):
                        row = jnp.broadcast_to(diag_ref[d + BLOCK, b : b + 1, lanes], (SUBLANES, LANES))
                        tiles[b] = jnp.where(here, row, tiles[b])
            for b in range(blocks):
                dense_ref[b, top : top + SUBLANES, lanes] = tiles[b]

    pairs = [split(product(split(dense_ref[b]), split(dense_ref[b + 1]))) for b in range(0, blocks, 2)]
    early = product(pairs[0], pairs[1])
    keep_ref[4 * rows : 4 * rows + width] = early
    early = split(early)
    late = split(product(pairs[2], pairs[3]))
    pack_ref[0:width] = product(early, late).astype(pack_ref.dtype)

    copies[2].wait()
    channels = feat_ref.shape[1]
    zero = jnp.zeros((channels, width), jnp.float32)
    first, second = sweep((zero, zero), feat_ref, keep_ref, rows // 2)
    keep_ref[4 * rows + width : 4 * rows + width + channels] = first
    high, low = split(second + product(split(first), late))
    pack_ref[width : width + channels] = high
    pack_ref[width + channels : width + 2 * channels] = low


def summary(features, mixing, decay_rate):
    rows, channels, width = features.shape
    vmem = pl.BlockSpec(memory_space=pltpu.VMEM)
    return pl.pallas_call(
        summary_kernel,
        in_specs=[pl.BlockSpec(memory_space=pltpu.HBM)] * 3,
        out_specs=[vmem] * 2,
        out_shape=(
            jax.ShapeDtypeStruct((width + 2 * channels, width), jnp.bfloat16),
            jax.ShapeDtypeStruct((4 * rows + width + channels, width), jnp.float32),
        ),
        scratch_shapes=[
            pltpu.VMEM(mixing.shape, jnp.float32),
            pltpu.VMEM(decay_rate.shape, jnp.float32),
            pltpu.VMEM(features.shape, features.dtype),
            pltpu.SemaphoreType.DMA((3,)),
            pltpu.VMEM((3, width // LANES, rows, LANES), jnp.float32),
            pltpu.VMEM((2 * BLOCK + 1, rows // BLOCK, width), jnp.float32),
            pltpu.VMEM((rows // BLOCK, width, width), jnp.float32),
        ],
        cost_estimate=pl.CostEstimate(
            flops=14 * rows * channels * width, bytes_accessed=4 * rows * channels * width, transcendentals=0
        ),
        compiler_params=pltpu.CompilerParams(vmem_limit_bytes=SUMMARY_MIB * MIB),
        name="summary",
    )(mixing, decay_rate, features)


def applied(state, operator):
    both = jnp.dot(jnp.concatenate(split(state)), operator, preferred_element_type=jnp.float32)
    return both[: state.shape[0]] + both[state.shape[0] :]


def unpacked(ref, width, channels):
    high = ref[width : width + channels].astype(jnp.float32)
    return high + ref[width + channels : width + 2 * channels].astype(jnp.float32)


def gated_kernel(core_ref, *refs):
    hop_refs, refs = refs[:3], refs[3:]
    theirs_ref, keep_ref, feat_ref, gate_ref, out_ref = refs
    rows, channels, width = feat_ref.shape
    incoming = hop_refs[0][...] + hop_refs[1][...] + hop_refs[2][...]
    later = applied(incoming, theirs_ref[0:width]) + unpacked(theirs_ref, width, channels)
    incoming = jnp.where(core_ref[0] == 0, incoming, later)
    early = keep_ref[4 * rows : 4 * rows + width]
    second = keep_ref[4 * rows + width : 4 * rows + width + channels] + product(split(incoming), split(early))

    def take(row, state):
        gate = gate_ref[row].astype(jnp.float32)
        out_ref[row] = (state * (gate / (1.0 + jnp.exp(-gate)))).astype(out_ref.dtype)

    sweep((incoming, second), feat_ref, keep_ref, rows // 2, take)


def gated(core, starts, features, gate_input):
    rows, channels, width = features.shape
    vmem = pl.BlockSpec(memory_space=pltpu.VMEM)
    return pl.pallas_call(
        gated_kernel,
        in_specs=[pl.BlockSpec(memory_space=pltpu.SMEM)] + [vmem] * (len(starts) + 2),
        out_specs=vmem,
        out_shape=jax.ShapeDtypeStruct(features.shape, jnp.bfloat16),
        cost_estimate=pl.CostEstimate(
            flops=48 * rows * channels * width,
            bytes_accessed=24 * rows * channels * width,
            transcendentals=8 * rows * channels * width,
        ),
        compiler_params=pltpu.CompilerParams(vmem_limit_bytes=8 * MIB),
        name="gated",
    )(core, *starts, features, gate_input)


def project_kernel(weight_ref, gated_ref, out_ref, done_ref, sem_ref):
    peers, rows, channels, width = gated_ref.shape
    outs = weight_ref.shape[0]
    tile = outs // TILES
    copies = []
    for row in range(rows):
        here = gated_ref[:, row].reshape(peers * channels, width)
        for t in range(TILES):
            part = pl.ds(t * tile, tile)
            done_ref[row, part, :] = jnp.dot(
                weight_ref[part, :], here, preferred_element_type=jnp.float32
            ).astype(done_ref.dtype)
            copy = pltpu.make_async_copy(done_ref.at[row, part], out_ref.at[row, part], sem_ref.at[row, t])
            copy.start()
            copies.append(copy)
    for copy in copies:
        copy.wait()


def project(out_weight, gathered):
    _, rows, _, width = gathered.shape
    outs = out_weight.shape[0]
    return pl.pallas_call(
        project_kernel,
        in_specs=[pl.BlockSpec(memory_space=pltpu.VMEM)] * 2,
        out_specs=pl.BlockSpec(memory_space=pl.ANY),
        out_shape=jax.ShapeDtypeStruct((rows, outs, width), jnp.bfloat16),
        scratch_shapes=[
            pltpu.VMEM((rows, outs, width), jnp.bfloat16),
            pltpu.SemaphoreType.DMA((rows, TILES)),
        ],
        compiler_params=pltpu.CompilerParams(vmem_limit_bytes=8 * MIB),
        cost_estimate=pl.CostEstimate(
            flops=2 * rows * outs * outs * width, bytes_accessed=4 * outs * outs, transcendentals=0
        ),
        name="project",
    )(out_weight, gathered)


def shards(slabs, peers, features, mixing, decay_rate, gate_input, out_weight):
    rows, channels, width = features.shape
    core = lax.axis_index("rows") % 2
    first = core == 0

    def chip_to(value, *pairs):
        return lax.ppermute(value, "rows", [(2 * a + c, 2 * b + c) for a, b in pairs for c in range(2)])

    mine, keep = summary(features, mixing, decay_rate)
    theirs = lax.ppermute(mine, "rows", [(i, i ^ 1) for i in range(slabs)])
    earlier = jnp.where(first, mine, theirs)
    later = jnp.where(first, theirs, mine)
    op_0, op_1 = earlier[:width], later[:width]
    chip_end = applied(unpacked(earlier, width, channels), op_1) + unpacked(later, width, channels)
    composite = jnp.dot(op_0, op_1, preferred_element_type=jnp.float32).astype(jnp.bfloat16)
    before = chip_to(chip_end, (0, 1), (1, 2), (2, 3))
    operator_on = chip_to(composite, (2, 3))
    carried = applied(before, composite) + chip_end
    far = chip_to(carried, (1, 3))
    near = chip_to(carried, (1, 2))
    chip = lax.axis_index("rows") // 2
    last = applied(far, operator_on) + before
    zero = jnp.zeros_like(last)
    hops = (jnp.where(chip == 1, before, zero), near, jnp.where(chip == 3, last, zero))

    starts = (*hops, theirs, keep)
    mixed = gated(core.astype(jnp.int32).reshape(1), starts, features, gate_input)
    mixed = mixed.reshape(peers, rows // peers, channels, width)
    return project(out_weight, lax.all_to_all(mixed, "chan", split_axis=0, concat_axis=0, tiled=True))


def solution(mesh):
    in_specs = (
        P("rows", "chan", None),
        P(None, "rows", None),
        P("rows", None),
        P("rows", "chan", None),
        P(),
    )
    out_specs = P(("rows", "chan"), None, None)

    def whole(features, mixing, decay_rate, gate_input, out_weight):
        return shards(
            mesh.shape["rows"], mesh.shape["chan"], features, mixing, decay_rate, gate_input, out_weight
        )

    return jax.shard_map(whole, mesh=mesh, in_specs=in_specs, out_specs=out_specs, check_vma=False)
```

time: 83.2 us -> 85.4 us (1.026)
  the two profiles are of different devices: /device:TPU:56 before, /device:TPU:48 now
where the time goes in v2:
time: 85.4 us; the launch traced here: 85.1 us
  blocking collectives  48.9 us (57%)
  Pallas kernels  14.8 us (17%)
  starting transfers between devices  9.05 us (11%)
  waiting for transfers between devices  8.88 us (10%)
  other arithmetic  1.66 us (2%)
  local copies, waits for them, and re-layouts  1.09 us (1%)
    all_to_all x1, blocking collectives, shards(): lax.all_to_all(mixed, 'chan', split_axis=0, concat_axis=0, tiled=True)  48.9 us
    ppermute x4, starting transfers between devices, chip_to(): lax.ppermute(value, 'rows', [(2 * a + c, 2 * b + c) for a, b in pairs for...  8.96 us
    pallas_call x1, Pallas kernels, summary(): pl.pallas_call(summary_kernel, in_specs=[pl.BlockSpec(memory_space=pltpu....  7.82 us
    ppermute x4, waiting for transfers between devices, chip_to(): lax.ppermute(value, 'rows', [(2 * a + c, 2 * b + c) for a, b in pairs for...  7.28 us
    pallas_call x1, Pallas kernels, gated(): pl.pallas_call(gated_kernel, in_specs=[pl.BlockSpec(memory_space=pltpu.SM...  3.54 us
    pallas_call x1, Pallas kernels, project(): pl.pallas_call(project_kernel, in_specs=[pl.BlockSpec(memory_space=pltpu....  3.46 us
  transfers between devices with their start and end apart: 5, of which 4 were waited for; matrix products, arithmetic and copies ran while one was open for 0% of the time, Pallas kernels for 0%

profile of v2, /device:TPU:48, one launch (start us, length us, event | category | flops | bytes accessed | tf_op | source)
XLA Modules:
  0.0 85.1 jit_solution(5111686602157809633)
XLA Ops:
  0.0 0.0 copy-start.1
  0.0 7.8 %summary.1 = (bf16[352,256]{1,0:T(8,128)(2,1)}, f32[560,256]{1,0:T(8,128)}) custom-call(f32[3,64,256]{2,1,0:T(8,128)} %mix_hbm.1, f32[64,256]{1,0:T(8,128)} %decay_hbm.1, bf16[64,48,256]{2,1,0:T(8,128)(2,1)} %refs_5_.1), custom_call_target="tpu_custom_call" | custom-call | flops 11010048 | bytes 3145728 | tf_op jit(solution)/shard_map/summary/pallas_call | solution.py:146
  7.8 0.0 copy-start
  7.8 0.1 collective-permute-start
  8.0 1.6 %collective-permute-done.refs_3_ = bf16[352,256]{1,0:T(8,128)(2,1)S(1)} collective-permute-done((bf16[352,256]{1,0:T(8,128)(2,1)}, bf16[352,256]{1,0:T(8,128)(2,1)S(1)}, u32[]{:S(2)}, u32[]{:S(2)}) %collective-permute-start) | collective-permute-done | bytes 180256 | tf_op jit(solution)/shard_map/ppermute | solution.py:264
  9.6 0.9 %broadcast_select_fusion.1 = (bf16[352,256]{1,0:T(8,128)(2,1)S(1)}, bf16[352,256]{1,0:T(8,128)(2,1)S(1)}) fusion(bf16[352,256]{1,0:T(8,128)(2,1)} %get-tuple-element.7, bf16[352,256]{1,0:T(8,128)(2,1)S(1)} %collective-permute-done.refs_3_, pred[]{:T(512)S(6)} %eq.12), kind=kLoop, calls=%fused_computation.2 | loop fusion | flops 180224 | bytes 720897 | tf_op jit(solution)/shard_map/jit(_where)/select_n | solution.py:265
  10.5 0.1 fusion.2
  10.7 3.2 %collective-permute-start.1 = (f32[48,256]{1,0:T(8,128)S(1)}, f32[48,256]{1,0:T(8,128)S(1)}, u32[]{:S(2)}, u32[]{:S(2)}) collective-permute-start(f32[48,256]{1,0:T(8,128)S(1)} %fusion.7), channel_id=1, source_target_pairs={{0,64},{32,96},{64,128},{96,160},{128,192},{160,224},{1,65},{33,97... | collective-permute-start | bytes 147464 | tf_op jit(solution)/shard_map/ppermute | solution.py:261
  13.9 0.2 convolution_convert_fusion
  14.1 2.6 %collective-permute-done.1 = f32[48,256]{1,0:T(8,128)S(1)} collective-permute-done((f32[48,256]{1,0:T(8,128)S(1)}, f32[48,256]{1,0:T(8,128)S(1)}, u32[]{:S(2)}, u32[]{:S(2)}) %collective-permute-start.1) | collective-permute-done | bytes 49184 | tf_op jit(solution)/shard_map/ppermute | solution.py:261
  16.7 0.1 fusion.11
  16.8 0.6 fusion.6
  17.5 0.7 collective-permute-start.3
  18.2 3.8 %collective-permute-start.4 = (bf16[256,256]{1,0:T(8,128)(2,1)S(1)}, bf16[256,256]{1,0:T(8,128)(2,1)S(1)}, u32[]{:S(2)}, u32[]{:S(2)}) collective-permute-start(bf16[256,256]{1,0:T(8,128)(2,1)S(1)} %convolution_convert_fusion), channel_id=1, source_target_pairs={{128,192},{160,224},{129,193},{161,225},{130,194},{162,226},{131,1... | collective-permute-start | bytes 393224 | tf_op jit(solution)/shard_map/ppermute | solution.py:261
  22.0 1.3 %collective-permute-start.2 = (f32[48,256]{1,0:T(8,128)}, f32[48,256]{1,0:T(8,128)S(1)}, u32[]{:S(2)}, u32[]{:S(2)}) collective-permute-start(f32[48,256]{1,0:T(8,128)} %fusion.6), channel_id=1, source_target_pairs={{64,128},{96,160},{65,129},{97,161},{66,130},{98,162},{67,131},{99... | collective-permute-start | bytes 147464 | tf_op jit(solution)/shard_map/ppermute | solution.py:261
  23.3 0.0 collective-permute-done.3
  23.3 1.2 %collective-permute-done.4 = bf16[256,256]{1,0:T(8,128)(2,1)S(1)} collective-permute-done((bf16[256,256]{1,0:T(8,128)(2,1)S(1)}, bf16[256,256]{1,0:T(8,128)(2,1)S(1)}, u32[]{:S(2)}, u32[]{:S(2)}) %collective-permute-start.4) | collective-permute-done | bytes 131104 | tf_op jit(solution)/shard_map/ppermute | solution.py:261
  24.5 0.1 fusion.15
  24.6 0.0 slice-start
  24.7 3.5 %collective-permute-done.2.refs_1_ = f32[48,256]{1,0:T(8,128)S(1)} collective-permute-done((f32[48,256]{1,0:T(8,128)}, f32[48,256]{1,0:T(8,128)S(1)}, u32[]{:S(2)}, u32[]{:S(2)}) %collective-permute-start.2) | collective-permute-done | bytes 49184 | tf_op jit(solution)/shard_map/ppermute | solution.py:261
  28.2 0.0 copy-done.1
  28.2 0.0 copy-done
  28.2 0.0 copy-start.2
  28.2 1.1 %copy-done.2 = f32[560,256]{1,0:T(8,128)S(1)} copy-done((f32[560,256]{1,0:T(8,128)S(1)}, f32[560,256]{1,0:T(8,128)}, u32[]{:S(2)}) %copy-start.2) | copy-done | bytes 573464
  29.3 0.0 slice-start.1
  29.3 3.5 %gated.1 = bf16[64,48,256]{2,1,0:T(8,128)(2,1)S(1)} custom-call(s32[1]{0:T(128)} %bitcast.core_ref, f32[48,256]{1,0:T(8,128)S(1)} %get-tuple-element.18.refs_0_, f32[48,256]{1,0:T(8,128)S(1)} %collective-permute-done.2.refs_1_, f32[48,256]{1,0:T(8,128)S(1)} %get-tuple-element.17.refs_2_, bf16[352,256]{1,0:T(8,128)(2,1)S(1)} %collective-permute-done.refs_3_, ...), custom_call_target="tpu_custom_call" | custom-call | flops 37748736 | bytes 18874368 | tf_op jit(solution)/shard_map/gated/pallas_call | solution.py:201
  32.8 48.9 %all_to_all.5.gated_ref = bf16[32,2,48,256]{3,2,1,0:T(8,128)(2,1)S(1)} all-to-all(bf16[32,2,48,256]{3,2,1,0:T(8,128)(2,1)S(1)} %bitcast.4), channel_id=1, replica_groups=mesh['rows'=8,'chan'=32] {'chan'}, dimensions={0} | all-to-all | bytes 3145728 | tf_op jit(solution)/shard_map/all_to_all | solution.py:283
  81.7 0.0 slice-done
  81.7 0.0 slice-done.1
  81.7 3.5 %project.1 = bf16[2,1536,256]{2,1,0:T(8,128)(2,1)} custom-call(bf16[1536,1536]{1,0:T(8,128)(2,1)S(1)} %bitcast.6, bf16[32,2,48,256]{3,2,1,0:T(8,128)(2,1)S(1)} %all_to_all.5.gated_ref), custom_call_target="tpu_custom_call" | custom-call | flops 2415919104 | bytes 9437184 | tf_op jit(solution)/shard_map/project/pallas_call | solution.py:238
  (6 shorter events, 0.1 us)
Async XLA Ops:
  0.0 28.2 %copy-start.1 = (bf16[64,48,256]{2,1,0:T(8,128)(2,1)S(1)}, bf16[64,48,256]{2,1,0:T(8,128)(2,1)}, u32[]{:S(2)}) copy-start(bf16[64,48,256]{2,1,0:T(8,128)(2,1)} %refs_6_.1) | copy-start | bytes 4718596
  7.8 20.4 %copy-start = (bf16[64,48,256]{2,1,0:T(8,128)(2,1)S(1)}, bf16[64,48,256]{2,1,0:T(8,128)(2,1)}, u32[]{:S(2)}) copy-start(bf16[64,48,256]{2,1,0:T(8,128)(2,1)} %refs_5_.1) | copy-start | bytes 4718596
  7.8 1.7 %collective-permute-start = (bf16[352,256]{1,0:T(8,128)(2,1)}, bf16[352,256]{1,0:T(8,128)(2,1)S(1)}, u32[]{:S(2)}, u32[]{:S(2)}) collective-permute-start(bf16[352,256]{1,0:T(8,128)(2,1)} %get-tuple-element.7), channel_id=1, source_target_pairs={{0,32},{32,0},{64,96},{96,64},{128,160},{160,128},{192,224},{224,1... | collective-permute-start | bytes 540680 | tf_op jit(solution)/shard_map/ppermute | solution.py:264
  10.7 6.0 %collective-permute-start.1 = (f32[48,256]{1,0:T(8,128)S(1)}, f32[48,256]{1,0:T(8,128)S(1)}, u32[]{:S(2)}, u32[]{:S(2)}) collective-permute-start(f32[48,256]{1,0:T(8,128)S(1)} %fusion.7), channel_id=1, source_target_pairs={{0,64},{32,96},{64,128},{96,160},{128,192},{160,224},{1,65},{33,97... | collective-permute-start | bytes 147464 | tf_op jit(solution)/shard_map/ppermute | solution.py:261
  17.5 5.8 %collective-permute-start.3 = (f32[48,256]{1,0:T(8,128)}, f32[48,256]{1,0:T(8,128)S(1)}, u32[]{:S(2)}, u32[]{:S(2)}) collective-permute-start(f32[48,256]{1,0:T(8,128)} %fusion.6), channel_id=1, source_target_pairs={{64,192},{96,224},{65,193},{97,225},{66,194},{98,226},{67,195},{99... | collective-permute-start | bytes 147464 | tf_op jit(solution)/shard_map/ppermute | solution.py:261
  18.2 6.3 %collective-permute-start.4 = (bf16[256,256]{1,0:T(8,128)(2,1)S(1)}, bf16[256,256]{1,0:T(8,128)(2,1)S(1)}, u32[]{:S(2)}, u32[]{:S(2)}) collective-permute-start(bf16[256,256]{1,0:T(8,128)(2,1)S(1)} %convolution_convert_fusion), channel_id=1, source_target_pairs={{128,192},{160,224},{129,193},{161,225},{130,194},{162,226},{131,1... | collective-permute-start | bytes 393224 | tf_op jit(solution)/shard_map/ppermute | solution.py:261
  22.0 6.2 %collective-permute-start.2 = (f32[48,256]{1,0:T(8,128)}, f32[48,256]{1,0:T(8,128)S(1)}, u32[]{:S(2)}, u32[]{:S(2)}) collective-permute-start(f32[48,256]{1,0:T(8,128)} %fusion.6), channel_id=1, source_target_pairs={{64,128},{96,160},{65,129},{97,161},{66,130},{98,162},{67,131},{99... | collective-permute-start | bytes 147464 | tf_op jit(solution)/shard_map/ppermute | solution.py:261
  24.6 57.0 %slice-start = ((s8[4718592]{0:T(1024)(128)(4,1)}), s8[4194304]{0:T(1024)(128)(4,1)S(1)}, s32[]{:S(2)}) async-start(s8[4718592]{0:T(1024)(128)(4,1)} %bitcast.5), calls=%async_computation.1 | async-start | bytes 8388608
  28.2 1.1 %copy-start.2 = (f32[560,256]{1,0:T(8,128)S(1)}, f32[560,256]{1,0:T(8,128)}, u32[]{:S(2)}) copy-start(f32[560,256]{1,0:T(8,128)} %get-tuple-element.8.refs_4_) | copy-start | bytes 1720324
  29.3 52.4 %slice-start.1 = ((s8[4718592]{0:T(1024)(128)(4,1)}), s8[524288]{0:T(1024)(128)(4,1)S(1)}, s32[]{:S(2)}) async-start(s8[4718592]{0:T(1024)(128)(4,1)} %bitcast.5), calls=%async_computation.2 | async-start | bytes 1048576

commit v3 on v2

--- a/solution.py
+++ b/solution.py
@@ -11,7 +11,6 @@
 LANES = 128
 TILES = 4
 MIB = 1024 * 1024
-SUMMARY_MIB = 62
 
 
 def stencil(state, left_w, mid_w, right_w):
@@ -50,13 +49,13 @@
 
 
 def summary_kernel(
-    mix_hbm, decay_hbm, feat_hbm, pack_ref, keep_ref,
-    mix_ref, decay_ref, feat_ref, sem_ref, side_ref, diag_ref, dense_ref,
+    _, mix_hbm, decay_hbm, feat_hbm, gate_hbm, pack_ref, keep_ref, feat_ref, gate_ref,
+    mix_ref, decay_ref, sem_ref, side_ref, diag_ref, dense_ref,
 ):
     copies = [
         pltpu.make_async_copy(source, target, sem_ref.at[k])
         for k, (source, target) in enumerate(
-            ((mix_hbm, mix_ref), (decay_hbm, decay_ref), (feat_hbm, feat_ref))
+            ((mix_hbm, mix_ref), (decay_hbm, decay_ref), (feat_hbm, feat_ref), (gate_hbm, gate_ref))
         )
     ]
     for copy in copies:
@@ -138,34 +137,36 @@
     high, low = split(second + product(split(first), late))
     pack_ref[width : width + channels] = high
     pack_ref[width + channels : width + 2 * channels] = low
-
-
-def summary(features, mixing, decay_rate):
+    copies[3].wait()
+
+
+def summary(place, features, gate_input, mixing, decay_rate):
     rows, channels, width = features.shape
     vmem = pl.BlockSpec(memory_space=pltpu.VMEM)
     return pl.pallas_call(
         summary_kernel,
-        in_specs=[pl.BlockSpec(memory_space=pltpu.HBM)] * 3,
-        out_specs=[vmem] * 2,
+        in_specs=[pl.BlockSpec(memory_space=pltpu.SMEM)] + [pl.BlockSpec(memory_space=pltpu.HBM)] * 4,
+        out_specs=[vmem] * 4,
         out_shape=(
-            jax.ShapeDtypeStruct((width + 2 * channels, width), jnp.bfloat16),
-            jax.ShapeDtypeStruct((4 * rows + width + channels, width), jnp.float32),
+            pltpu.VMEM((width + 2 * channels, width), jnp.bfloat16),
+            pltpu.VMEM((4 * rows + width + channels, width), jnp.float32),
+            pltpu.VMEM(features.shape, features.dtype),
+            pltpu.VMEM(gate_input.shape, gate_input.dtype),
         ),
         scratch_shapes=[
             pltpu.VMEM(mixing.shape, jnp.float32),
             pltpu.VMEM(decay_rate.shape, jnp.float32),
-            pltpu.VMEM(features.shape, features.dtype),
-            pltpu.SemaphoreType.DMA((3,)),
+            pltpu.SemaphoreType.DMA((4,)),
             pltpu.VMEM((3, width // LANES, rows, LANES), jnp.float32),
             pltpu.VMEM((2 * BLOCK + 1, rows // BLOCK, width), jnp.float32),
             pltpu.VMEM((rows // BLOCK, width, width), jnp.float32),
         ],
         cost_estimate=pl.CostEstimate(
-            flops=14 * rows * channels * width, bytes_accessed=4 * rows * channels * width, transcendentals=0
-        ),
-        compiler_params=pltpu.CompilerParams(vmem_limit_bytes=SUMMARY_MIB * MIB),
+            flops=14 * rows * channels * width, bytes_accessed=26 * MIB, transcendentals=0
+        ),
+        compiler_params=pltpu.CompilerParams(vmem_limit_bytes=16 * MIB),
         name="summary",
-    )(mixing, decay_rate, features)
+    )(place, *[pltpu.with_memory_space_constraint(a, pltpu.HBM) for a in (mixing, decay_rate, features, gate_input)])
 
 
 def applied(state, operator):
@@ -178,13 +179,71 @@
     return high + ref[width + channels : width + 2 * channels].astype(jnp.float32)
 
 
-def gated_kernel(core_ref, *refs):
-    hop_refs, refs = refs[:3], refs[3:]
-    theirs_ref, keep_ref, feat_ref, gate_ref, out_ref = refs
+def chip_kernel(place_ref, mine_ref, theirs_ref, on_ref, end_ref):
+    channels, width = end_ref.shape
+
+    def write(earlier_ref, later_ref):
+        later_op = later_ref[0:width]
+        end = applied(unpacked(earlier_ref, width, channels), later_op) + unpacked(later_ref, width, channels)
+        end_ref[...] = end
+        high, low = split(end)
+        on_ref[width : width + channels] = high
+        on_ref[width + channels : width + 2 * channels] = low
+        both = jnp.dot(earlier_ref[0:width], later_op, preferred_element_type=jnp.float32)
+        on_ref[0:width] = both.astype(on_ref.dtype)
+
+    @pl.when(place_ref[0] == 0)
+    def _():
+        write(mine_ref, theirs_ref)
+
+    @pl.when(place_ref[0] != 0)
+    def _():
+        write(theirs_ref, mine_ref)
+
+
+def chip_of(place, mine, theirs):
+    width = mine.shape[1]
+    channels = (mine.shape[0] - width) // 2
+    vmem = pl.BlockSpec(memory_space=pltpu.VMEM)
+    return pl.pallas_call(
+        chip_kernel,
+        in_specs=[pl.BlockSpec(memory_space=pltpu.SMEM), vmem, vmem],
+        out_specs=(vmem, vmem),
+        out_shape=(
+            jax.ShapeDtypeStruct(mine.shape, mine.dtype),
+            jax.ShapeDtypeStruct((channels, width), jnp.float32),
+        ),
+        cost_estimate=pl.CostEstimate(flops=2 * width**3, bytes_accessed=4 * MIB, transcendentals=0),
+        compiler_params=pltpu.CompilerParams(vmem_limit_bytes=4 * MIB),
+        name="chip",
+    )(place, mine, theirs)
+
+
+def carry_kernel(before_ref, on_ref, end_ref, out_ref):
+    out_ref[...] = applied(before_ref[...], on_ref[0 : out_ref.shape[1]]) + end_ref[...]
+
+
+def carry(before, on, chip_end):
+    vmem = pl.BlockSpec(memory_space=pltpu.VMEM)
+    return pl.pallas_call(
+        carry_kernel,
+        in_specs=[vmem] * 3,
+        out_specs=vmem,
+        out_shape=jax.ShapeDtypeStruct(chip_end.shape, jnp.float32),
+        cost_estimate=pl.CostEstimate(flops=2 * on.size, bytes_accessed=2 * MIB, transcendentals=0),
+        compiler_params=pltpu.CompilerParams(vmem_limit_bytes=4 * MIB),
+        name="carry",
+    )(before, on, chip_end)
+
+
+def gated_kernel(
+    place_ref, before_ref, near_ref, far_ref, beyond_ref, theirs_ref, keep_ref, feat_ref, gate_ref, out_ref
+):
     rows, channels, width = feat_ref.shape
-    incoming = hop_refs[0][...] + hop_refs[1][...] + hop_refs[2][...]
+    farther = applied(far_ref[...], beyond_ref[0:width]) + unpacked(beyond_ref, width, channels)
+    incoming = before_ref[...] + near_ref[...] + farther
     later = applied(incoming, theirs_ref[0:width]) + unpacked(theirs_ref, width, channels)
-    incoming = jnp.where(core_ref[0] == 0, incoming, later)
+    incoming = jnp.where(place_ref[0] == 0, incoming, later)
     early = keep_ref[4 * rows : 4 * rows + width]
     second = keep_ref[4 * rows + width : 4 * rows + width + channels] + product(split(incoming), split(early))
 
@@ -195,7 +254,7 @@
     sweep((incoming, second), feat_ref, keep_ref, rows // 2, take)
 
 
-def gated(core, starts, features, gate_input):
+def gated(place, starts, features, gate_input):
     rows, channels, width = features.shape
     vmem = pl.BlockSpec(memory_space=pltpu.VMEM)
     return pl.pallas_call(
@@ -210,7 +269,7 @@
         ),
         compiler_params=pltpu.CompilerParams(vmem_limit_bytes=8 * MIB),
         name="gated",
-    )(core, *starts, features, gate_input)
+    )(place, *starts, features, gate_input)
 
 
 def project_kernel(weight_ref, gated_ref, out_ref, done_ref, sem_ref):
@@ -254,31 +313,23 @@
 
 def shards(slabs, peers, features, mixing, decay_rate, gate_input, out_weight):
     rows, channels, width = features.shape
-    core = lax.axis_index("rows") % 2
-    first = core == 0
+    place = lax.axis_index("rows").astype(jnp.int32)
+    place = jnp.stack([place % 2, place // 2])
 
     def chip_to(value, *pairs):
         return lax.ppermute(value, "rows", [(2 * a + c, 2 * b + c) for a, b in pairs for c in range(2)])
 
-    mine, keep = summary(features, mixing, decay_rate)
+    mine, keep, features, gate_input = summary(place, features, gate_input, mixing, decay_rate)
     theirs = lax.ppermute(mine, "rows", [(i, i ^ 1) for i in range(slabs)])
-    earlier = jnp.where(first, mine, theirs)
-    later = jnp.where(first, theirs, mine)
-    op_0, op_1 = earlier[:width], later[:width]
-    chip_end = applied(unpacked(earlier, width, channels), op_1) + unpacked(later, width, channels)
-    composite = jnp.dot(op_0, op_1, preferred_element_type=jnp.float32).astype(jnp.bfloat16)
-    before = chip_to(chip_end, (0, 1), (1, 2), (2, 3))
-    operator_on = chip_to(composite, (2, 3))
-    carried = applied(before, composite) + chip_end
+    on, chip_end = chip_of(place, mine, theirs)
+    before = chip_to(chip_end, (0, 1))
+    beyond = chip_to(on, (2, 3))
+    carried = carry(before, on, chip_end)
     far = chip_to(carried, (1, 3))
     near = chip_to(carried, (1, 2))
-    chip = lax.axis_index("rows") // 2
-    last = applied(far, operator_on) + before
-    zero = jnp.zeros_like(last)
-    hops = (jnp.where(chip == 1, before, zero), near, jnp.where(chip == 3, last, zero))
-
-    starts = (*hops, theirs, keep)
-    mixed = gated(core.astype(jnp.int32).reshape(1), starts, features, gate_input)
+
+    starts = (before, near, far, beyond, theirs, keep)
+    mixed = gated(place, starts, features, gate_input)
     mixed = mixed.reshape(peers, rows // peers, channels, width)
     return project(out_weight, lax.all_to_all(mixed, "chan", split_axis=0, concat_axis=0, tiled=True))
 

time: 85.4 us -> 79.4 us (0.930)
  starting transfers between devices: 9.05 us -> 6.17 us
  waiting for transfers between devices: 8.88 us -> 7.29 us
  other arithmetic: 1.66 us -> 0.08 us
  Pallas kernels: 14.8 us -> 16.2 us
  local copies, waits for them, and re-layouts: 1.09 us -> 0.01 us
    ppermute x4, starting transfers between devices: 8.96 us -> 6.08 us  [chip_to(): lax.ppermute(value, 'rows', [(2 * a + c, 2 * b + c) for a, b in pairs for...]
    ppermute x4, waiting for transfers between devices: 7.28 us -> 5.88 us  [chip_to(): lax.ppermute(value, 'rows', [(2 * a + c, 2 * b + c) for a, b in pairs for...]
    unnamed x10 -> x4, local copies, waits for them, and re-layouts: 1.09 us -> 0.01 us
    select_n x2 -> x0, other arithmetic: 0.96 us -> none  [the longest x1 0.95 us: shards(): earlier = jnp.where(first, mine, theirs)]
    pallas_call x0 -> x2, Pallas kernels: none -> 0.92 us  [the longest x1 0.76 us: chip_of(): pl.pallas_call(chip_kernel, in_specs=[pl.BlockSpec(memory_space=pltpu.SME...]
  transfers between devices with their start and end apart: 5 -> 5, of which waited for: 4 -> 2; matrix products, arithmetic and copies ran while one was open for 0% -> 0% of each run, Pallas kernels for 0% -> 0%
where the time goes in v3:
time: 79.4 us; the launch traced here: 79.2 us
  blocking collectives  49.4 us (62%)
  Pallas kernels  16.2 us (20%)
  waiting for transfers between devices  7.29 us (9%)
  starting transfers between devices  6.17 us (8%)
    all_to_all x1, blocking collectives, shards(): lax.all_to_all(mixed, 'chan', split_axis=0, concat_axis=0, tiled=True)  49.4 us
    pallas_call x1, Pallas kernels, summary(): pl.pallas_call(summary_kernel, in_specs=[pl.BlockSpec(memory_space=pltpu....  7.58 us
    ppermute x4, starting transfers between devices, chip_to(): lax.ppermute(value, 'rows', [(2 * a + c, 2 * b + c) for a, b in pairs for...  6.08 us
    ppermute x4, waiting for transfers between devices, chip_to(): lax.ppermute(value, 'rows', [(2 * a + c, 2 * b + c) for a, b in pairs for...  5.88 us
    pallas_call x1, Pallas kernels, gated(): pl.pallas_call(gated_kernel, in_specs=[pl.BlockSpec(memory_space=pltpu.SM...  4.24 us
    pallas_call x1, Pallas kernels, project(): pl.pallas_call(project_kernel, in_specs=[pl.BlockSpec(memory_space=pltpu....  3.47 us
  transfers between devices with their start and end apart: 5, of which 2 were waited for; matrix products, arithmetic and copies ran while one was open for 0% of the time, Pallas kernels for 0%

profile of v3, /device:TPU:48, one launch (start us, length us, event | category | flops | bytes accessed | tf_op | source)
XLA Modules:
  0.0 79.2 jit_solution(3128257496093252719)
XLA Ops:
  0.0 0.1 pad_add_fusion._.place_ref
  0.1 7.6 %summary.1 = (bf16[352,256]{1,0:T(8,128)(2,1)S(1)}, f32[560,256]{1,0:T(8,128)S(1)}, bf16[64,48,256]{2,1,0:T(8,128)(2,1)S(1)}, bf16[64,48,256]{2,1,0:T(8,128)(2,1)S(1)}) custom-call(s32[2]{0:T(128)S(1)} %pad_add_fusion._.place_ref, f32[3,64,256]{2,1,0:T(8,128)} %mix_hbm.1, f32[64,256]{1,0:T(8,128)} %decay_hbm.1, bf16[64,48,256]{2,1,0:T(8,128)(2,1)} %feat_hbm.1, ...), custom_call_target="tpu_custom_call" | custom-call | flops 11010048 | bytes 27262976 | tf_op jit(solution)/shard_map/summary/pallas_call | solution.py:146
  7.7 0.1 collective-permute-start
  7.8 1.4 %collective-permute-done.theirs_ref = bf16[352,256]{1,0:T(8,128)(2,1)S(1)} collective-permute-done((bf16[352,256]{1,0:T(8,128)(2,1)S(1)}, bf16[352,256]{1,0:T(8,128)(2,1)S(1)}, u32[]{:S(2)}, u32[]{:S(2)}) %collective-permute-start) | collective-permute-done | bytes 180256 | tf_op jit(solution)/shard_map/ppermute | solution.py:323
  9.2 0.8 chip.1
  9.9 3.2 %collective-permute-start.4 = (bf16[352,256]{1,0:T(8,128)(2,1)S(1)}, bf16[352,256]{1,0:T(8,128)(2,1)S(1)}, u32[]{:S(2)}, u32[]{:S(2)}) collective-permute-start(bf16[352,256]{1,0:T(8,128)(2,1)S(1)} %get-tuple-element.13.on_ref), channel_id=1, source_target_pairs={{128,192},{160,224},{129,193},{161,225},{130,194},{162,226},{131,1... | collective-permute-start | bytes 540680 | tf_op jit(solution)/shard_map/ppermute | solution.py:320
  13.1 0.7 collective-permute-start.1
  13.8 0.0 collective-permute-done.1.before_ref
  13.8 0.0 slice-start
  13.8 0.2 carry.1
  14.0 0.8 %collective-permute-start.3 = (f32[48,256]{1,0:T(8,128)S(1)}, f32[48,256]{1,0:T(8,128)S(1)}, u32[]{:S(2)}, u32[]{:S(2)}) collective-permute-start(f32[48,256]{1,0:T(8,128)S(1)} %carry.1), channel_id=1, source_target_pairs={{64,192},{96,224},{65,193},{97,225},{66,194},{98,226},{67,195},{99... | collective-permute-start | bytes 147464 | tf_op jit(solution)/shard_map/ppermute | solution.py:320
  14.8 1.4 %collective-permute-start.2 = (f32[48,256]{1,0:T(8,128)S(1)}, f32[48,256]{1,0:T(8,128)S(1)}, u32[]{:S(2)}, u32[]{:S(2)}) collective-permute-start(f32[48,256]{1,0:T(8,128)S(1)} %carry.1), channel_id=1, source_target_pairs={{64,128},{96,160},{65,129},{97,161},{66,130},{98,162},{67,131},{99... | collective-permute-start | bytes 147464 | tf_op jit(solution)/shard_map/ppermute | solution.py:320
  16.2 0.0 collective-permute-done.3.far_ref
  16.2 5.9 %collective-permute-done.2.near_ref = f32[48,256]{1,0:T(8,128)S(1)} collective-permute-done((f32[48,256]{1,0:T(8,128)S(1)}, f32[48,256]{1,0:T(8,128)S(1)}, u32[]{:S(2)}, u32[]{:S(2)}) %collective-permute-start.2) | collective-permute-done | bytes 49184 | tf_op jit(solution)/shard_map/ppermute | solution.py:320
  22.1 0.0 collective-permute-done.4.beyond_ref
  22.1 0.0 slice-start.1
  22.1 4.2 %gated.1 = bf16[64,48,256]{2,1,0:T(8,128)(2,1)S(1)} custom-call(s32[2]{0:T(128)S(1)} %pad_add_fusion._.place_ref, f32[48,256]{1,0:T(8,128)S(1)} %collective-permute-done.1.before_ref, f32[48,256]{1,0:T(8,128)S(1)} %collective-permute-done.2.near_ref, f32[48,256]{1,0:T(8,128)S(1)} %collective-permute-done.3.far_ref, ...), custom_call_target="tpu_custom_call" | custom-call | flops 37748736 | bytes 18874368 | tf_op jit(solution)/shard_map/gated/pallas_call | solution.py:260
  26.4 49.4 %all_to_all.5.gated_ref = bf16[32,2,48,256]{3,2,1,0:T(8,128)(2,1)S(1)} all-to-all(bf16[32,2,48,256]{3,2,1,0:T(8,128)(2,1)S(1)} %bitcast.3), channel_id=1, replica_groups=mesh['rows'=8,'chan'=32] {'chan'}, dimensions={0} | all-to-all | bytes 3145728 | tf_op jit(solution)/shard_map/all_to_all | solution.py:334
  75.8 0.0 slice-done
  75.8 0.0 slice-done.1
  75.8 3.5 %project.1 = bf16[2,1536,256]{2,1,0:T(8,128)(2,1)} custom-call(bf16[1536,1536]{1,0:T(8,128)(2,1)S(1)} %bitcast.5, bf16[32,2,48,256]{3,2,1,0:T(8,128)(2,1)S(1)} %all_to_all.5.gated_ref), custom_call_target="tpu_custom_call" | custom-call | flops 2415919104 | bytes 9437184 | tf_op jit(solution)/shard_map/project/pallas_call | solution.py:297
  (1 shorter events, 0.0 us)
Async XLA Ops:
  7.7 1.5 %collective-permute-start = (bf16[352,256]{1,0:T(8,128)(2,1)S(1)}, bf16[352,256]{1,0:T(8,128)(2,1)S(1)}, u32[]{:S(2)}, u32[]{:S(2)}) collective-permute-start(bf16[352,256]{1,0:T(8,128)(2,1)S(1)} %get-tuple-element.11.mine_ref), channel_id=1, source_target_pairs={{0,32},{32,0},{64,96},{96,64},{128,160},{160,128},{192,224},{224,1... | collective-permute-start | bytes 540680 | tf_op jit(solution)/shard_map/ppermute | solution.py:323
  9.9 12.2 %collective-permute-start.4 = (bf16[352,256]{1,0:T(8,128)(2,1)S(1)}, bf16[352,256]{1,0:T(8,128)(2,1)S(1)}, u32[]{:S(2)}, u32[]{:S(2)}) collective-permute-start(bf16[352,256]{1,0:T(8,128)(2,1)S(1)} %get-tuple-element.13.on_ref), channel_id=1, source_target_pairs={{128,192},{160,224},{129,193},{161,225},{130,194},{162,226},{131,1... | collective-permute-start | bytes 540680 | tf_op jit(solution)/shard_map/ppermute | solution.py:320
  13.1 0.7 collective-permute-start.1
  13.8 61.9 %slice-start = ((s8[4718592]{0:T(1024)(128)(4,1)}), s8[4194304]{0:T(1024)(128)(4,1)S(1)}, s32[]{:S(2)}) async-start(s8[4718592]{0:T(1024)(128)(4,1)} %bitcast.4), calls=%async_computation.1 | async-start | bytes 8388608
  14.0 2.2 %collective-permute-start.3 = (f32[48,256]{1,0:T(8,128)S(1)}, f32[48,256]{1,0:T(8,128)S(1)}, u32[]{:S(2)}, u32[]{:S(2)}) collective-permute-start(f32[48,256]{1,0:T(8,128)S(1)} %carry.1), channel_id=1, source_target_pairs={{64,192},{96,224},{65,193},{97,225},{66,194},{98,226},{67,195},{99... | collective-permute-start | bytes 147464 | tf_op jit(solution)/shard_map/ppermute | solution.py:320
  14.8 7.3 %collective-permute-start.2 = (f32[48,256]{1,0:T(8,128)S(1)}, f32[48,256]{1,0:T(8,128)S(1)}, u32[]{:S(2)}, u32[]{:S(2)}) collective-permute-start(f32[48,256]{1,0:T(8,128)S(1)} %carry.1), channel_id=1, source_target_pairs={{64,128},{96,160},{65,129},{97,161},{66,130},{98,162},{67,131},{99... | collective-permute-start | bytes 147464 | tf_op jit(solution)/shard_map/ppermute | solution.py:320
  22.1 53.6 %slice-start.1 = ((s8[4718592]{0:T(1024)(128)(4,1)}), s8[524288]{0:T(1024)(128)(4,1)S(1)}, s32[]{:S(2)}) async-start(s8[4718592]{0:T(1024)(128)(4,1)} %bitcast.4), calls=%async_computation.2 | async-start | bytes 1048576
